TPU v7x, 128 devices: a whole 4x4x4 slice. The times are simulated.
128 devices in a mesh: pool: 16 (over x, z), rep: 8 (over y, core).
Axes of the slice: x: 4, y: 4, z: 4, core: 2. Of those that a mesh axis runs over, the one named last changes fastest.
Arguments:
- hidden: bfloat16 [8, 64, 2048], P('rep', 'pool'), may hold values from -6 to 6
- queries: bfloat16 [8, 64, 16, 192], P('rep', 'pool'), may hold values from -8 to 8
- new_kv: bfloat16 [8, 64, 576], P('rep', 'pool'), may hold values from -6 to 6
- kv_cache: bfloat16 [8, 768, 128, 576], P('rep', 'pool'), may hold values from -8 to 8
- block_table: int32 [8, 64, 128], P('rep'), may hold values from -1 to 767, as said below
- seq_lens: int32 [8, 64], P('rep'), may hold values from 1 to 16384, as said below
- w_uk: bfloat16 [16, 128, 512], replicated, may hold values from -0.5 to 0.5
- w_uv: bfloat16 [16, 512, 128], replicated, may hold values from -0.25 to 0.25
- o_proj: bfloat16 [2048, 2048], P('rep'), may hold values from -0.125 to 0.125
- norm_gain: float32 [2048], replicated, may hold values from 0.1 to 1.9
- routes: int32 [16, 8, 4, 6], P('pool'), may hold values from 0 to 63, all different within a row; in each aligned block of 32 rows (0 to 31, 32 to 63, ..., all dimensions but the last counted through in order) at most 6 rows name the same one
- gate_weights: float32 [16, 8, 4, 6], P('pool'), may hold values from 0.02 to 0.3
- w_gate: bfloat16 [64, 2048, 1408], P('pool', None, 'rep'), may hold values from -0.125 to 0.125
- w_up: bfloat16 [64, 2048, 1408], P('pool', None, 'rep'), may hold values from -0.125 to 0.125
- w_down: bfloat16 [64, 1408, 2048], P('pool', 'rep'), may hold values from -0.15625 to 0.15625
- shared_gate: bfloat16 [2048, 2816], P(None, 'rep'), may hold values from -0.125 to 0.125
- shared_up: bfloat16 [2048, 2816], P(None, 'rep'), may hold values from -0.125 to 0.125
- shared_down: bfloat16 [2816, 2048], P('rep'), may hold values from -0.109375 to 0.109375
Outputs:
- attn_out: bfloat16 [8, 64, 2048], P('rep', 'pool')
- layer_out: bfloat16 [8, 64, 2048], P('rep', 'pool')
Inputs may be any that keep to these rules, and one draw needn't show every extreme that they name: `block_table`: entry (g, j, i) for i < ceil(seq_lens[g, j] / 128) names a page p of group g's 768 pages, page p lying on pool index p // 48; these pages are all different within a group; the other entries are -1. `seq_lens`: in every group one request has 16384 cached tokens. Each row names 6 different experts; among the 32 rows routes[p] of one pool index no expert is named more than 6 times.
All inputs are finite; a program needn't handle non-finite values.
Results may differ from a plain program's by a relative error of at most 0.02.
Values may be sent and summed in bfloat16 or wider, within the bound.
A program may use at most 128 MiB of HBM per device.

v0:
```python
import jax
import jax.numpy as jnp
from jax import lax
from jax.sharding import PartitionSpec as P

very_negative = -1e30
norm_eps = 1e-06
highest = lax.Precision.HIGHEST


def swiglu(rows_in, gate_w, up_w, down_w):
    gate_act = jnp.dot(rows_in, gate_w, preferred_element_type=jnp.float32)
    up_act = jnp.dot(rows_in, up_w, preferred_element_type=jnp.float32)
    inner_act = (jax.nn.silu(gate_act) * up_act).astype(jnp.bfloat16)
    return jnp.dot(inner_act, down_w, preferred_element_type=jnp.float32)


def shards(
    hidden,
    queries,
    new_kv,
    kv_cache,
    block_table,
    seq_lens,
    w_uk,
    w_uv,
    o_proj,
    norm_gain,
    routes,
    gate_weights,
    w_gate,
    w_up,
    w_down,
    shared_gate,
    shared_up,
    shared_down,
):
    rows_own = hidden.shape[1]
    model_width = hidden.shape[2]
    head_count = queries.shape[2]
    qk_width = queries.shape[3]
    nope_width = w_uk.shape[1]
    latent_width = w_uk.shape[2]
    value_width = w_uv.shape[2]
    pages_local = kv_cache.shape[1]
    page_len = kv_cache.shape[2]
    pool_size = lax.axis_size("pool")
    pool_rank = lax.axis_index("pool")
    rep_rank = lax.axis_index("rep")
    scaling = qk_width ** (-0.5)
    query_own = queries[0]
    fresh_own = new_kv[0]
    cache_own = kv_cache[0]
    page_table = block_table[0]
    lengths = seq_lens[0]
    absorbed = jnp.einsum(
        "khn,hnl->khl", query_own[..., :nope_width], w_uk, preferred_element_type=jnp.float32
    )
    fanned = (
        jnp.concatenate([absorbed, query_own[..., nope_width:].astype(jnp.float32)], axis=-1)
        * scaling
    ).astype(jnp.bfloat16)
    all_queries = lax.all_gather(fanned, "pool", axis=0, tiled=True)
    group_size = all_queries.shape[0]
    slot_ids = jnp.arange(page_table.shape[1], dtype=jnp.int32)
    counts = (lengths + page_len - 1) // page_len
    local_ids = page_table - pool_rank * pages_local
    is_mine = (slot_ids[None, :] < counts[:, None]) & (local_ids >= 0) & (local_ids < pages_local)
    target = jnp.where(is_mine, local_ids, pages_local).reshape(-1)
    request_ids = jnp.broadcast_to(
        jnp.arange(group_size, dtype=jnp.int32)[:, None], page_table.shape
    ).reshape(-1)
    place_ids = jnp.broadcast_to(slot_ids[None, :], page_table.shape).reshape(-1)
    owner_req = jnp.zeros((pages_local,), jnp.int32).at[target].set(request_ids, mode="drop")
    place_of = jnp.zeros((pages_local,), jnp.int32).at[target].set(place_ids, mode="drop")
    is_used = (
        jnp.zeros((pages_local,), jnp.int32).at[target].set(jnp.ones_like(request_ids), mode="drop")
        == 1
    )
    tokens = place_of[:, None] * page_len + jnp.arange(page_len, dtype=jnp.int32)[None, :]
    is_valid = is_used[:, None] & (tokens < lengths[owner_req][:, None])
    scores = jnp.einsum(
        "ihc,itc->iht", all_queries[owner_req], cache_own, preferred_element_type=jnp.float32
    )
    masked = jnp.where(is_valid[:, None, :], scores, very_negative)
    member = (owner_req[None, :] == jnp.arange(group_size, dtype=jnp.int32)[:, None]) & is_used[
        None, :
    ]
    page_peak = jnp.max(masked, axis=-1)
    local_peak = jnp.max(
        jnp.where(member[:, :, None], page_peak[None, :, :], very_negative), axis=1
    )
    own_score = jnp.einsum("khc,kc->kh", fanned, fresh_own, preferred_element_type=jnp.float32)
    own_start = pool_rank * rows_own
    own_peak = lax.dynamic_slice_in_dim(local_peak, own_start, rows_own, 0)
    local_peak = lax.dynamic_update_slice_in_dim(
        local_peak, jnp.maximum(own_peak, own_score), own_start, 0
    )
    peak_used = lax.pmax(local_peak, "pool")
    weights = jnp.where(
        is_valid[:, None, :], jnp.exp(masked - peak_used[owner_req][:, :, None]), 0.0
    ).astype(jnp.bfloat16)
    page_numer = jnp.einsum(
        "iht,itl->ihl", weights, cache_own[..., :latent_width], preferred_element_type=jnp.float32
    )
    member_f = member.astype(jnp.float32)
    numerator = jnp.einsum("ji,ihl->jhl", member_f, page_numer, precision=highest)
    denominator = jnp.einsum(
        "ji,ih->jh", member_f, jnp.sum(weights.astype(jnp.float32), axis=-1), precision=highest
    )
    own_round = jnp.exp(
        own_score - lax.dynamic_slice_in_dim(peak_used, own_start, rows_own, 0)
    ).astype(jnp.bfloat16)
    own_weight = lax.optimization_barrier(own_round).astype(jnp.float32)
    own_numer = own_weight[:, :, None] * fresh_own[:, None, :latent_width].astype(jnp.float32)
    numerator = lax.dynamic_update_slice_in_dim(
        numerator,
        lax.dynamic_slice_in_dim(numerator, own_start, rows_own, 0) + own_numer,
        own_start,
        0,
    )
    denominator = lax.dynamic_update_slice_in_dim(
        denominator,
        lax.dynamic_slice_in_dim(denominator, own_start, rows_own, 0) + own_weight,
        own_start,
        0,
    )
    value_map = w_uv.astype(jnp.float32)
    numer_own, denom_own = (
        lax.psum_scatter(
            numerator.astype(jnp.bfloat16), "pool", scatter_dimension=0, tiled=True
        ).astype(jnp.float32),
        lax.psum_scatter(
            denominator.astype(jnp.bfloat16), "pool", scatter_dimension=0, tiled=True
        ).astype(jnp.float32),
    )
    head_sum = jnp.einsum("khl,hlv->khv", numer_own, value_map, precision=highest)
    head_values = (
        (head_sum / denom_own[:, :, None])
        .astype(jnp.bfloat16)
        .reshape(rows_own, head_count * value_width)
    )
    column_heads = lax.all_gather(head_values, "rep", axis=0, tiled=True)
    block_rows = o_proj.shape[0]
    head_block = lax.dynamic_slice_in_dim(column_heads, rep_rank * block_rows, block_rows, 1)
    attn_proj = lax.psum_scatter(
        jnp.dot(head_block, o_proj, preferred_element_type=jnp.float32).astype(jnp.bfloat16),
        "rep",
        scatter_dimension=0,
        tiled=True,
    ).astype(jnp.float32)
    residual = hidden[0].astype(jnp.float32) + attn_proj
    normed = (
        residual
        * lax.rsqrt(jnp.mean(residual * residual, axis=-1, keepdims=True) + norm_eps)
        * norm_gain
    ).astype(jnp.bfloat16)
    column_x = lax.all_gather(normed, "rep", axis=0, tiled=True)
    column_count = column_x.shape[0]
    top_count = routes.shape[3]
    experts_here = w_gate.shape[0]
    experts_all = experts_here * pool_size
    capacity = max(2, column_count * top_count * 2 // experts_all)
    flat_ids = routes[0].reshape(-1)
    flat_gates = gate_weights[0].reshape(-1)
    one_hot = (flat_ids[:, None] == jnp.arange(experts_all, dtype=jnp.int32)[None, :]).astype(
        jnp.int32
    )
    slot_of = jnp.sum(jnp.cumsum(one_hot, axis=0) * one_hot, axis=1) - 1
    source_row = jnp.arange(column_count * top_count, dtype=jnp.int32) // top_count
    dispatch = (
        jnp.zeros((experts_all, capacity, model_width), jnp.bfloat16)
        .at[flat_ids, slot_of]
        .set(column_x[source_row])
    )
    dispatch = dispatch.reshape(pool_size, experts_here, capacity, model_width)
    incoming = lax.all_to_all(dispatch, "pool", split_axis=0, concat_axis=0, tiled=True)
    gate_act = jnp.einsum("pecd,edf->pecf", incoming, w_gate, preferred_element_type=jnp.float32)
    up_act = jnp.einsum("pecd,edf->pecf", incoming, w_up, preferred_element_type=jnp.float32)
    inner_act = (jax.nn.silu(gate_act) * up_act).astype(jnp.bfloat16)
    slice_out = jnp.einsum("pecf,efd->pecd", inner_act, w_down, preferred_element_type=jnp.float32)
    returned = lax.all_to_all(
        slice_out.astype(jnp.bfloat16), "pool", split_axis=0, concat_axis=0, tiled=True
    ).astype(slice_out.dtype)
    feature_count = returned.shape[3]
    returned_rows = returned.reshape(experts_all * capacity, feature_count)
    picked = returned_rows[flat_ids * capacity + slot_of] * flat_gates[:, None]
    routed = jnp.sum(picked.reshape(column_count, top_count, feature_count), axis=1)
    moe_sum = lax.psum_scatter(
        (swiglu(column_x, shared_gate, shared_up, shared_down) + routed).astype(jnp.bfloat16),
        "rep",
        scatter_dimension=0,
        tiled=True,
    ).astype(jnp.float32)
    layer_out = (residual + moe_sum).astype(jnp.bfloat16)
    return (attn_proj.astype(jnp.bfloat16)[None], layer_out[None])


def solution(mesh):
    placed = (
        P("rep", "pool", None),
        P("rep", "pool", None, None),
        P("rep", "pool", None),
        P("rep", "pool", None, None),
        P("rep", None, None),
        P("rep", None),
        P(),
        P(),
        P("rep", None),
        P(),
        P("pool", None, None, None),
        P("pool", None, None, None),
        P("pool", None, "rep"),
        P("pool", None, "rep"),
        P("pool", "rep", None),
        P(None, "rep"),
        P(None, "rep"),
        P("rep", None),
    )
    return jax.shard_map(
        shards,
        mesh=mesh,
        in_specs=placed,
        out_specs=(P("rep", "pool", None), P("rep", "pool", None)),
        check_vma=False,
    )
```

profile of v0, /device:TPU:1, one launch (start us, length us, event | category | flops | bytes accessed | tf_op | source)
XLA Modules:
  0.0 533.1 jit_solution(6518522593258579567)
XLA Ops:
  7.3 0.9 copy.158
  8.2 2.0 convolution_bitcast_fusion
  10.2 0.6 copy.95
  11.1 0.1 compare_select_fusion
  11.2 30.4 %scatter_custom_fusion = s32[48]{0:T(128)S(1)} fusion(s32[8192]{0:T(1024)S(1)} %bitcast.148, s32[8192]{0:T(1024)S(1)} %iota_bitcast_fusion.1, s32[]{:T(128)} %constant.27.clone.1), kind=kCustom, calls=%fused_computation.134 | custom fusion | bytes 196 | tf_op jit(solution)/shard_map/scatter | solution.py:74
  41.7 30.4 %scatter_custom_fusion.1 = s32[48]{0:T(128)S(1)} fusion(s32[8192]{0:T(1024)S(1)} %bitcast.149, s32[8192]{0:T(1024)S(1)} %broadcast.336, s32[]{:T(128)} %constant.27.clone.1), kind=kCustom, calls=%fused_computation.132 | custom fusion | bytes 196 | tf_op jit(solution)/shard_map/scatter | solution.py:77
  72.1 30.4 %scatter_custom_fusion.2 = s32[48]{0:T(128)S(1)} fusion(s32[8192]{0:T(1024)S(1)} %bitcast.150, s32[8192]{0:T(1024)S(1)} %iota_bitcast_fusion, s32[]{:T(128)} %constant.27.clone.1), kind=kCustom, calls=%fused_computation.130 | custom fusion | bytes 196 | tf_op jit(solution)/shard_map/scatter | solution.py:75
  102.6 0.1 fusion.77
  102.8 10.5 %copy.96 = bf16[1,48,128,576]{3,2,1,0:T(8,128)(2,1)} copy(bf16[1,48,128,576]{2,3,1,0:T(8,128)(2,1)} %param.21) | data formatting | bytes 14155776 | tf_op args[3]
  113.3 0.8 gather_fusion
  114.3 3.0 gather_fusion.1
  117.3 4.5 fusion.96
  121.8 0.2 select_reduce_fusion
  122.1 0.2 dynamic_update_slice.9
  122.3 35.9 %pmax.7 = f32[64,16]{0,1:T(8,128)S(1)} all-reduce(f32[64,16]{0,1:T(8,128)S(1)} %dynamic_update_slice.9), channel_id=1, replica_groups=mesh['pool'=16,'rep'=8] {'pool'}, use_global_device_ids=true, to_apply=%region_5.6 | all-reduce | flops 1024 | bytes 8192 | tf_op jit(solution)/shard_map/pmax | solution.py:99
  158.3 0.6 gather_fusion.2
  158.9 3.8 fusion.2
  162.7 2.1 fusion.17
  164.9 0.1 add_dynamic-update-slice_fusion
  165.0 0.1 convert_element_type.83
  165.2 1.6 copy.100
  166.8 0.1 copy.102
  166.9 0.1 eq.50
  167.0 0.1 reshape_squeeze.3
  167.2 0.6 dynamic-slice
  167.8 0.6 dynamic-slice.2
  169.7 0.6 reduce-window.6
  170.3 0.2 slice_reduce_fusion
  170.7 0.3 convert_reduce_fusion
  171.0 0.2 fusion.93
  171.3 0.2 dynamic_update_slice.11
  171.5 28.6 %all-reduce.1 = bf16[64,16]{0,1:T(8,128)(2,1)S(1)} all-reduce(bf16[64,16]{0,1:T(8,128)(2,1)S(1)} %convert_element_type.85), channel_id=3, replica_groups=mesh['pool'=16,'rep'=8] {'pool'}, use_global_device_ids=true, to_apply=%region_8.9.clone | all-reduce | flops 1024 | bytes 4096
  200.2 41.9 %reduce-scatter.3.cloned.1.call-done = bf16[4,16,512]{2,1,0:T(8,128)(2,1)} async-done(((bf16[64,16,512]{2,1,0:T(8,128)(2,1)}), bf16[4,16,512]{2,1,0:T(8,128)(2,1)}) %reduce-scatter.3.cloned.1.call-update) | async-done | bytes 65552 | tf_op jit(solution)/shard_map/reduce_scatter | solution.py:130
  242.1 2.0 fusion.47
  244.1 15.3 %all-gather = bf16[8,4,2048]{2,1,0:T(4,128)(2,1)S(1)} all-gather(bf16[1,4,2048]{2,1,0:T(4,128)(2,1)S(1)} %fusion.47), channel_id=1, replica_groups=mesh['pool'=16,'rep'=8] {'rep'}, dimensions={0}, use_global_device_ids=true | all-gather | bytes 147456 | tf_op jit(solution)/shard_map/all_gather | solution.py:143
  259.5 2.2 convolution_convert_fusion
  261.7 55.5 %all-reduce.7.cloned.1.call-done = bf16[32,2048]{1,0:T(8,128)(2,1)} async-done(((bf16[32,2048]{1,0:T(8,128)(2,1)}), bf16[32,2048]{1,0:T(8,128)(2,1)}) %all-reduce.7.cloned.1.call-update) | async-done | bytes 131088
  317.2 0.9 multiply_reduce_fusion.1
  318.1 0.8 fusion.73
  319.0 15.3 %all-gather.1 = bf16[8,4,2048]{2,1,0:T(4,128)(2,1)S(1)} all-gather(bf16[1,4,2048]{2,1,0:T(4,128)(2,1)S(1)} %fusion.73), channel_id=1, replica_groups=mesh['pool'=16,'rep'=8] {'rep'}, dimensions={0}, use_global_device_ids=true | all-gather | bytes 147456 | tf_op jit(solution)/shard_map/all_gather | solution.py:158
  334.4 2.0 gather_fusion.3
  336.4 1.3 broadcast_in_dim.62
  337.7 35.1 %scatter_fusion = bf16[64,6,2048]{2,0,1:T(8,128)(2,1)} fusion(bf16[64,6,2048]{2,0,1:T(8,128)(2,1)} %broadcast_in_dim.62, s32[192]{0:T(256)S(1)} %bitcast.143, bf16[192,2048]{1,0:T(8,128)(2,1)} %gather_fusion.3), kind=kCustom, calls=%fused_computation.8 | custom fusion | bytes 2360832 | tf_op jit(solution)/shard_map/scatter | solution.py:174
  372.8 3.6 reshape.329
  376.5 2.1 copy.106
  378.6 28.2 %all_to_all.10 = bf16[16,4,6,2048]{3,1,2,0:T(4,128)(2,1)S(1)} all-to-all(bf16[16,4,6,2048]{3,1,2,0:T(4,128)(2,1)S(1)} %copy.106), channel_id=1, replica_groups=mesh['pool'=16,'rep'=8] {'pool'}, dimensions={0} | all-to-all | bytes 3145728 | tf_op jit(solution)/shard_map/all_to_all | solution.py:177
  406.8 1.1 copy-done.2
  408.0 2.1 fusion.21
  410.0 5.3 fusion.13
  415.3 3.8 copy.109
  419.1 4.5 all-to-all-start.1
  423.6 0.3 all-reduce.9.cloned.1.call-start
  424.0 1.9 fusion.97
  425.9 18.1 %all-to-all-done.1 = bf16[16,4,6,2048]{3,1,2,0:T(4,128)(2,1)} async-done(((bf16[16,4,6,2048]{3,1,2,0:T(4,128)(2,1)}), bf16[16,4,6,2048]{3,1,2,0:T(4,128)(2,1)}, u32[]{:S(2)}, u32[]{:S(2)}) %all-to-all-start.1) | async-done | bytes 1572896 | tf_op jit(solution)/shard_map/all_to_all | solution.py:182
  443.9 2.3 copy_convert_fusion
  446.3 3.8 copy.111
  450.1 4.8 reshape.335
  454.8 4.9 gather_fusion.4
  459.7 2.7 gather.22
  462.4 2.3 multiply_reduce_fusion
  464.8 3.6 fusion.16
  468.4 1.4 dynamic-slice_bitcast_fusion
  469.7 55.4 %all-reduce.9.cloned.1.call-done = bf16[32,2048]{1,0:T(8,128)(2,1)} async-done(((bf16[32,2048]{1,0:T(8,128)(2,1)}), bf16[32,2048]{1,0:T(8,128)(2,1)}) %all-reduce.9.cloned.1.call-update) | async-done | bytes 131088
  525.2 1.4 fusion.74
  (68 shorter events, 1.5 us)
Async XLA Ops:
  7.2 402.9 %copy-start = (bf16[4,176,2048]{2,1,0:T(8,128)(2,1)S(1)}, bf16[4,176,2048]{2,1,0:T(8,128)(2,1)}, u32[]{:S(2)}) copy-start(bf16[4,176,2048]{2,1,0:T(8,128)(2,1)} %param.32) | copy-start | bytes 8650756
  7.2 3.8 copy-start.1
  7.2 3.9 copy-start.4
  7.2 95.4 %copy-start.8 = (bf16[1,4,576]{2,1,0:T(4,128)(2,1)S(1)}, bf16[1,4,576]{2,1,0:T(4,128)(2,1)}, u32[]{:S(2)}) copy-start(bf16[1,4,576]{2,1,0:T(4,128)(2,1)} %param.20) | copy-start | bytes 13828
  7.2 107.1 %all-gather.4.cloned.1.call-start = ((), (), s32[]{:S(2)}) async-start(), calls=%async_computation.3 | async-start | bytes 1392640 | tf_op jit(solution)/shard_map/all_gather | solution.py:63
  10.9 231.2 %reduce-scatter.3.cloned.1.call-start = ((), (), s32[]{:S(2)}) async-start(), calls=%async_computation.4 | async-start | bytes 1114112 | tf_op jit(solution)/shard_map/reduce_scatter | solution.py:130
  165.1 1.7 copy-start.5
  165.1 2.0 copy-start.11
  165.2 2.6 copy-start.10
  166.8 150.5 %all-reduce.7.cloned.1.call-start = ((), (), s32[]{:S(2)}) async-start(), calls=%async_computation.5 | async-start | bytes 262144
  200.2 117.1 %copy-start.3 = (bf16[1,4,2048]{2,1,0:T(4,128)(2,1)S(1)}, bf16[1,4,2048]{2,1,0:T(4,128)(2,1)}, u32[]{:S(2)}) copy-start(bf16[1,4,2048]{2,1,0:T(4,128)(2,1)} %param.18) | copy-start | bytes 49156
  200.2 118.0 %copy-start.7 = (f32[2048]{0:T(1024)S(1)}, f32[2048]{0:T(1024)}, u32[]{:S(2)}) copy-start(f32[2048]{0:T(1024)} %param.27) | copy-start | bytes 24580
  378.6 29.3 %copy-start.9 = (bf16[4,2048,176]{1,2,0:T(8,128)(2,1)S(1)}, bf16[4,2048,176]{1,2,0:T(8,128)(2,1)}, u32[]{:S(2)}) copy-start(bf16[4,2048,176]{1,2,0:T(8,128)(2,1)} %param.30) | copy-start | bytes 8650756
  406.8 1.1 copy-start.2
  419.1 4.8 copy-start.6
  419.1 24.9 %all-to-all-start.1 = ((bf16[16,4,6,2048]{3,1,2,0:T(4,128)(2,1)}), bf16[16,4,6,2048]{3,1,2,0:T(4,128)(2,1)}, u32[]{:S(2)}, u32[]{:S(2)}) async-start(bf16[16,4,6,2048]{3,1,2,0:T(4,128)(2,1)} %copy.109), calls=%async_computation.2 | async-start | bytes 3145728 | tf_op jit(solution)/shard_map/all_to_all | solution.py:182
  423.6 101.6 %all-reduce.9.cloned.1.call-start = ((), (), s32[]{:S(2)}) async-start(), calls=%async_computation.6 | async-start | bytes 262144
Sparse Core Ops, SparseCore 0:
  11.0 45.8 all-gather.3
  166.9 75.2 reduce-scatter.2
  261.8 55.3 all-reduce.6
  468.5 56.6 all-reduce.8
where the time goes:
time: 537 us; the launch traced here: 533 us
  local copies, waits for them, and re-layouts  178 us (33%)
  waiting for transfers between devices  171 us (32%)
  blocking collectives  123 us (23%)
  matrix products  29.7 us (6%)
  between operations  15.5 us (3%)
  other arithmetic  10.1 us (2%)
    unnamed x6, waiting for transfers between devices  111 us
    scatter x2, local copies, waits for them, and re-layouts, shards(): jnp.zeros((pages_local,), jnp.int32).at[target]  60.9 us
    reduce_scatter x1, waiting for transfers between devices, shards(): lax.psum_scatter(numerator.astype(jnp.bfloat16), 'pool', scatter_dimensio...  41.9 us
    pmax x1, blocking collectives, shards(): peak_used = lax.pmax(local_peak, 'pool')  35.9 us
    scatter x1, local copies, waits for them, and re-layouts, shards(): dispatch = jnp.zeros((experts_all, capacity, model_width), jnp.bfloat16)....  35.1 us
    scatter x1, local copies, waits for them, and re-layouts, shards(): jnp.zeros((pages_local,), jnp.int32).at[target].set(place_ids, mode='drop')  30.4 us
    unnamed x1, blocking collectives  28.6 us
    all_to_all x1, blocking collectives, shards(): lax.all_to_all(dispatch, 'pool', split_axis=0, concat_axis=0, tiled=True)  28.2 us
  transfers between devices with their start and end apart: 5, of which 4 were waited for; matrix products, arithmetic and copies ran while one was open for 21% of the time, Pallas kernels for 0%

commit v1 on v0

v1 whole, which is shorter than its diff:
```python
import functools

import jax
import jax.numpy as jnp
from jax import lax
from jax.experimental import pallas as pl
from jax.experimental.pallas import tpu as pltpu
from jax.sharding import PartitionSpec as P

F32 = jnp.float32
BF16 = jnp.bfloat16
NEG = -1e30
EPS = 1e-06
NX = 4
MESH = pl.DeviceIdType.MESH
VM = pl.BlockSpec(memory_space=pltpu.VMEM)
HBM = pl.BlockSpec(memory_space=pl.ANY)
SM = pl.BlockSpec(memory_space=pltpu.SMEM)
NT = (((1,), (1,)), ((), ()))
LIMIT = 60 * 1024 * 1024


def dot(a, b):
    return jnp.dot(a, b, preferred_element_type=F32)


def dot_nt(a, b):
    return lax.dot_general(a, b, NT, preferred_element_type=F32)


def place():
    p = lax.axis_index("pool")
    r = lax.axis_index("rep")
    return p // NX, p % NX, r // 2, r % 2


def pool_peers(x, z):
    out = []
    for d in range(1, 16):
        dx, dz = d // 4, d % 4
        out.append((d, ((x + dx) % 4) * 4 + (z + dz) % 4))
    return out


def rep_peers(y, c):
    out = []
    for d in range(1, 8):
        dy, dc = d // 2, d % 2
        out.append((d, ((y + dy) % 4) * 2 + (c + dc) % 2))
    return out


def send(src, dst, ssem, rsem, pool=None, rep=None):
    dev = {}
    if pool is not None:
        dev["pool"] = pool
    if rep is not None:
        dev["rep"] = rep
    cp = pltpu.make_async_remote_copy(
        src_ref=src, dst_ref=dst, send_sem=ssem, recv_sem=rsem, device_id=dev, device_id_type=MESH
    )
    cp.start()
    return cp


def greet(pool_list, rep_list):
    bar = pltpu.get_barrier_semaphore()
    for _, q in pool_list:
        pl.semaphore_signal(bar, inc=1, device_id={"pool": q}, device_id_type=MESH)
    for _, q in rep_list:
        pl.semaphore_signal(bar, inc=1, device_id={"rep": q}, device_id_type=MESH)
    pl.semaphore_wait(bar, len(pool_list) + len(rep_list))


def gather_queries(q_ref, out_ref, ssem, rsem):
    x, z, y, c = place()
    me = x * 4 + z
    peers = pool_peers(x, z)
    greet(peers, [])
    cps = [send(q_ref, out_ref.at[me], ssem.at[d], rsem.at[d], pool=q) for d, q in peers]
    out_ref[me] = q_ref[...]
    for cp in cps:
        cp.wait()


def attention(
    meta, qg, wuk, wuv, cache, fresh, p_out, stat_out, kv, qf, fq, sb, lb, db, acc, of, sf, sem
):
    pages = 48
    chunk = 8
    scale = 192 ** (-0.5)
    loads = []
    for i in range(pages // chunk):
        s = pl.ds(i * chunk, chunk)
        cp = pltpu.make_async_copy(cache.at[s], kv.at[s], sem.at[i])
        cp.start()
        loads.append(cp)
    kv[pages] = fresh[...]

    @pl.loop(0, 64, unroll=4)
    def _(j):
        v = qg[j].astype(F32)
        s = pl.ds(pl.multiple_of(j * 16, 16), 16)
        qf[0, s, :] = v[:, 0:128]
        qf[1, s, 0:64] = v[:, 128:192]
        lb[s, :] = jnp.full((16, 128), NEG, F32)
        db[s, :] = jnp.zeros((16, 128), F32)
        for t in range(4):
            acc[t, s, :] = jnp.zeros((16, 128), F32)

    for h in range(16):
        s = pl.ds(h, 64, stride=16)
        qa = qf[0, s, :].astype(BF16)
        qb = qf[1, s, :]
        a = dot(qa, wuk[h]) * scale
        for t in range(4):
            fq[t, s, :] = a[:, t * 128 : (t + 1) * 128]
        fq[4, s, :] = qb * scale

    lane = lax.broadcasted_iota(jnp.int32, (16, 128), 1)

    def scores(i):
        j = meta[0, i]
        lo = meta[1, i]
        hi = meta[2, i]
        ik = jnp.minimum(i, pages)
        s = pl.ds(pl.multiple_of(j * 16, 16), 16)
        qa = jnp.concatenate([fq[t, s, :] for t in range(4)], axis=1).astype(BF16)
        qb = fq[4, s, :][:, 0:64].astype(BF16)
        v = dot(qa, kv[ik, 0:512, :]) + dot(qb, kv[ik, 512:576, :])
        v = jnp.where((lane >= lo) & (lane < hi), v, NEG)
        sb[i] = v
        m = jnp.broadcast_to(jnp.max(v, axis=1, keepdims=True), (16, 128))
        lb[s, :] = jnp.maximum(lb[s, :], m)

    def sums(i):
        j = meta[0, i]
        lo = meta[1, i]
        hi = meta[2, i]
        ik = jnp.minimum(i, pages)
        s = pl.ds(pl.multiple_of(j * 16, 16), 16)
        w = jnp.exp(sb[i] - lb[s, :])
        w = jnp.where((lane >= lo) & (lane < hi), w, 0.0).astype(BF16)
        den = jnp.sum(w.astype(F32), axis=1, keepdims=True)
        num = dot_nt(w, kv[ik, 0:512, :])
        db[s, :] = db[s, :] + jnp.broadcast_to(den, (16, 128))
        for t in range(4):
            acc[t, s, :] = acc[t, s, :] + num[:, t * 128 : (t + 1) * 128]

    for i in range(pages // chunk):
        loads[i].wait()

        @pl.loop(0, chunk // 4)
        def _(g, i=i):
            for u in range(4):
                scores(i * chunk + g * 4 + u)

    for u in range(4):
        scores(jnp.int32(pages + u))

    @pl.loop(0, (pages + 4) // 4)
    def _(g):
        for u in range(4):
            sums(g * 4 + u)

    lane64 = lax.broadcasted_iota(jnp.int32, (64, 128), 1)
    stat = jnp.zeros((64, 128), F32)
    for h in range(16):
        s = pl.ds(h, 64, stride=16)
        a = jnp.concatenate([acc[t, s, :] for t in range(4)], axis=1).astype(BF16)
        d = db[s, :]
        full = d > 0.0
        safe = jnp.where(full, d, 1.0)
        of[:, h * 128 : (h + 1) * 128] = dot(a, wuv[h]) / safe
        lse = jnp.where(full, lb[s, :] + jnp.log(safe), NEG)
        stat = jnp.where(lane64 == h, lse, stat)
    sf[...] = stat
    for d in range(16):
        p_out[d] = of[d * 4 : (d + 1) * 4, :].astype(BF16)
        stat_out[d] = sf[d * 4 : (d + 1) * 4, :]


WIDTHS = (384, 384, 256)
STARTS = (0, 384, 768)
ORDERS = (("x", "z", "y"), ("z", "y", "x"), ("y", "x", "z"))
AX = {"x": 0, "z": 1, "y": 2}


def rest(
    p_ref, st_ref, hid, gain, gates_in, oproj_h, wg_h, wu_h, wd_h, sg_h, su_h, sd_h,
    attn_out, layer_out,
    oproj, wg, wu, wd, sg, su, sd, wsem,
    rp, rst, gates, heads, hs, hb, hbf, pf, ps, pr, nown, npart, blk,
    x0, x1, x2, xm, inner, shin, y0, y1, y2, cs0, cs1, cs2, cr0, cr1, cr2,
    sb0, sb1, sb2, ra0, ra1, ra2, rb0, rb1, rb2, rc0, rc1, rc2,
    za0, za1, za2, zb0, zb1, zb2, fs, fr,
    psem, ssem, gsem, hsem, osem, nsem, asem, fsem, csem, rsem, lsem,
):
    x, z, y, c = place()
    me = x * 4 + z
    rp_me = y * 2 + c
    coord = {"x": x, "z": z, "y": y}
    pools = pool_peers(x, z)
    reps = rep_peers(y, c)
    mate = y * 2 + 1 - c
    xs = (x0, x1, x2)
    wl = []
    for i, (h, v) in enumerate(
        ((oproj_h, oproj), (sg_h, sg), (su_h, su), (sd_h, sd), (wg_h, wg), (wu_h, wu), (wd_h, wd))
    ):
        cp = pltpu.make_async_copy(h, v, wsem.at[i])
        cp.start()
        wl.append(cp)
    greet(pools, reps)

    sc = [send(st_ref.at[q], rst.at[me], ssem.at[0, d], ssem.at[1, d], pool=q) for d, q in pools]
    pc = [send(p_ref.at[q], rp.at[me], psem.at[0, d], psem.at[1, d], pool=q) for d, q in pools]
    gc = [send(gates_in, gates.at[me], gsem.at[0, d], gsem.at[1, d], pool=q) for d, q in pools]
    rst[me] = st_ref[me]
    rp[me] = p_ref[me]
    gates[me] = gates_in[...]
    for cp in sc:
        cp.wait()
    top = rst[0]
    for s in range(1, 16):
        top = jnp.maximum(top, rst[s])
    tot = jnp.zeros((4, 128), F32)
    for s in range(16):
        e = jnp.exp(rst[s] - top)
        rst[s] = e
        tot = tot + e
    inv = 1.0 / tot
    for cp in pc:
        cp.wait()

    heads[...] = jnp.zeros((4, 2048), F32)

    @pl.loop(0, 16)
    def _(s):
        w = rst[s] * inv
        for h in range(16):
            cols = slice(h * 128, (h + 1) * 128)
            heads[:, cols] = heads[:, cols] + w[:, h : h + 1] * rp[s, :, cols].astype(F32)

    for g in range(8):
        hs[g] = heads[:, g * 256 : (g + 1) * 256].astype(BF16)
    hc = [send(hs.at[q], hb.at[rp_me], hsem.at[0, d], hsem.at[1, d], rep=q) for d, q in reps]
    hb[rp_me] = hs[rp_me]
    wl[0].wait()
    for cp in hc:
        cp.wait()
    for g in range(8):
        hbf[g * 4 : (g + 1) * 4, :] = hb[g].astype(F32)
    pf[...] = dot(hbf[...].astype(BF16), oproj[...])
    for g in range(8):
        ps[g] = pf[g * 4 : (g + 1) * 4, :].astype(BF16)
    oc = [send(ps.at[q], pr.at[rp_me], osem.at[0, d], osem.at[1, d], rep=q) for d, q in reps]
    pr[rp_me] = ps[rp_me]
    for cp in oc:
        cp.wait()
    proj = pr[0].astype(F32)
    for g in range(1, 8):
        proj = proj + pr[g].astype(F32)
    attn_out[...] = proj.astype(BF16)
    res = hid[...].astype(F32) + proj
    ms = jnp.mean(res * res, axis=1, keepdims=True)
    normed = (res * lax.rsqrt(ms + EPS) * gain[...]).astype(BF16)

    nown[...] = normed
    cp = send(nown, npart, nsem.at[0], nsem.at[1], rep=mate)
    for g in gc:
        g.wait()
    cp.wait()
    mine = normed.astype(F32)
    theirs = npart[...].astype(F32)
    blk[0:4, :] = jnp.where(c == 0, mine, theirs)
    blk[4:8, :] = jnp.where(c == 0, theirs, mine)
    for t in range(3):
        for h in range(2):
            s = h * 1024 + STARTS[t]
            xs[t][h, x, z, y] = blk[:, s : s + WIDTHS[t]].astype(BF16)

    def region(t, stage, over=None):
        idx = [None, None, None]
        for s, a in enumerate(ORDERS[t]):
            if s < stage:
                idx[AX[a]] = pl.ds(0, 4)
            else:
                v = coord[a]
                if s == stage and over is not None:
                    v = (v + over) % 4
                idx[AX[a]] = pl.ds(v, 1)
        return tuple(idx)

    def peer(a, d):
        v = (coord[a] + d) % 4
        if a == "x":
            return {"pool": v * 4 + z}
        if a == "z":
            return {"pool": x * 4 + v}
        return {"rep": v * 2 + c}

    fwd = []
    moving = {}
    for stage in range(3):
        for t in range(3):
            if stage > 0:
                for d in range(1, 4):
                    moving[t, stage - 1, d].wait()
                    reg = (c,) + region(t, stage - 1, -d)
                    k = (stage - 1) * 3 + d - 1
                    fwd.append(
                        send(xs[t].at[reg], xs[t].at[reg], fsem.at[0, t, k], fsem.at[1, t, k], rep=mate)
                    )
            for d in range(1, 4):
                a = ORDERS[t][stage]
                reg = (c,) + region(t, stage)
                moving[t, stage, d] = send(
                    xs[t].at[reg], xs[t].at[reg],
                    asem.at[0, t, stage, d], asem.at[1, t, stage, d], **peer(a, d)
                )
    for t in range(3):
        for d in range(1, 4):
            moving[t, 2, d].wait()
            reg = (c,) + region(t, 2, -d)
            k = 6 + d - 1
            fwd.append(send(xs[t].at[reg], xs[t].at[reg], fsem.at[0, t, k], fsem.at[1, t, k], rep=mate))
    for cp in fwd:
        cp.wait()

    for t in range(3):
        for h in range(2):
            s = h * 1024 + STARTS[t]
            v = xs[t][h].astype(F32).reshape(512, WIDTHS[t]).astype(BF16)
            xm[:, s : s + WIDTHS[t]] = v

    for cp in wl[1:]:
        cp.wait()

    col = xm[pl.ds(pl.multiple_of(me * 32, 32), 32), :]
    ga = dot_nt(col, sg[...])
    ua = dot_nt(col, su[...])
    shin[...] = (ga / (1.0 + jnp.exp(-ga)) * ua).astype(BF16)

    gm = gates[...].reshape(512, 128)
    ids = lax.broadcasted_iota(jnp.int32, (128, 176), 0) % 64

    @pl.loop(0, 4)
    def _(e):
        ga = dot_nt(xm[...], wg[e])
        ua = dot_nt(xm[...], wu[e])
        gw = dot(gm, jnp.where(ids == me * 4 + e, 1.0, 0.0).astype(BF16))
        inner[e] = (ga / (1.0 + jnp.exp(-ga)) * ua * gw).astype(BF16)

    ys = (y0, y1, y2)
    css = (cs0, cs1, cs2)
    crs = (cr0, cr1, cr2)
    cc = []
    for mine_half in (False, True):
        half = c if mine_half else 1 - c
        for t in range(3):
            wdt = WIDTHS[t]
            cols = pl.ds(pl.multiple_of(half * 1024 + STARTS[t], 128), wdt)
            v = dot(inner[0], wd[0, :, cols])
            for e in range(1, 4):
                v = v + dot(inner[e], wd[e, :, cols])
            sh = dot(shin[...], sd[:, cols])
            ys[t][...] = v.reshape(4, 4, 4, 8, wdt)
            ys[t][x, z] = ys[t][x, z] + sh.reshape(4, 8, wdt)
            if not mine_half:
                css[t][...] = ys[t][...].astype(BF16)
                cc.append(send(css[t], crs[t], csem.at[0, t], csem.at[1, t], rep=mate))

    sbs = (sb0, sb1, sb2)
    ras, rbs, rcs = (ra0, ra1, ra2), (rb0, rb1, rb2), (rc0, rc1, rc2)
    zas, zbs = (za0, za1, za2), (zb0, zb1, zb2)

    def part(t, stage, at):
        idx = [None, None, None]
        for s, a in enumerate(ORDERS[t]):
            if s < stage:
                idx[AX[a]] = pl.ds(0, 4)
            elif s == stage:
                idx[AX[a]] = pl.ds(at, 1)
            else:
                idx[AX[a]] = pl.ds(0, 1)
        return tuple(idx)

    going = {}
    for t in range(3):
        cc[t].wait()
        tot = ys[t][...] + crs[t][...].astype(F32)
        ys[t][...] = tot
        sbs[t][...] = tot.astype(BF16)
        a = ORDERS[t][2]
        for d in range(1, 4):
            going[t, 2, d] = send(
                sbs[t].at[part(t, 2, (coord[a] + d) % 4)], ras[t].at[d],
                rsem.at[0, t, 2, d], rsem.at[1, t, 2, d], **peer(a, d)
            )
    for t in range(3):
        a = ORDERS[t][2]
        for d in range(1, 4):
            going[t, 2, d].wait()
        v = ys[t][part(t, 2, coord[a])]
        for d in range(1, 4):
            v = v + ras[t][d].astype(F32)
        ras[t][0] = v.astype(BF16)
        zas[t][...] = v
        a = ORDERS[t][1]
        for d in range(1, 4):
            going[t, 1, d] = send(
                ras[t].at[(0,) + part(t, 1, (coord[a] + d) % 4)], rbs[t].at[d],
                rsem.at[0, t, 1, d], rsem.at[1, t, 1, d], **peer(a, d)
            )
    for t in range(3):
        a = ORDERS[t][1]
        for d in range(1, 4):
            going[t, 1, d].wait()
        v = zas[t][part(t, 1, coord[a])]
        for d in range(1, 4):
            v = v + rbs[t][d].astype(F32)
        rbs[t][0] = v.astype(BF16)
        zbs[t][...] = v
        a = ORDERS[t][0]
        for d in range(1, 4):
            going[t, 0, d] = send(
                rbs[t].at[(0,) + part(t, 0, (coord[a] + d) % 4)], rcs[t].at[d],
                rsem.at[0, t, 0, d], rsem.at[1, t, 0, d], **peer(a, d)
            )
    for t in range(3):
        a = ORDERS[t][0]
        for d in range(1, 4):
            going[t, 0, d].wait()
        v = zbs[t][part(t, 0, coord[a])]
        for d in range(1, 4):
            v = v + rcs[t][d].astype(F32)
        blk[:, STARTS[t] : STARTS[t] + WIDTHS[t]] = v.reshape(8, WIDTHS[t])
    lo, hi = blk[0:4, 0:1024], blk[4:8, 0:1024]
    fs[...] = jnp.where(c == 0, hi, lo).astype(BF16)
    cp = send(fs, fr, lsem.at[0], lsem.at[1], rep=mate)
    own = jnp.where(c == 0, lo, hi)
    cp.wait()
    other = fr[...].astype(F32)
    layer_out[:, 0:1024] = (res[:, 0:1024] + jnp.where(c == 0, own, other)).astype(BF16)
    layer_out[:, 1024:2048] = (res[:, 1024:2048] + jnp.where(c == 0, other, own)).astype(BF16)


def dma(*shape):
    return pltpu.SemaphoreType.DMA(shape)


def rest_scratch():
    v = pltpu.VMEM
    out = [
        v((256, 2048), BF16), v((4, 176, 2048), BF16), v((4, 176, 2048), BF16), v((4, 176, 2048), BF16),
        v((352, 2048), BF16), v((352, 2048), BF16), v((352, 2048), BF16), dma(7),
        v((16, 4, 2048), BF16), v((16, 4, 128), F32), v((16, 32, 128), BF16), v((4, 2048), F32),
        v((8, 4, 256), BF16), v((8, 4, 256), BF16), v((32, 256), F32), v((32, 2048), F32),
        v((8, 4, 2048), BF16), v((8, 4, 2048), BF16), v((4, 2048), BF16), v((4, 2048), BF16),
        v((8, 2048), F32),
    ]
    out += [v((2, 4, 4, 4, 8, w), BF16) for w in WIDTHS]
    out += [v((512, 2048), BF16), v((4, 512, 176), BF16), v((32, 352), BF16)]
    out += [v((4, 4, 4, 8, w), F32) for w in WIDTHS]
    out += [v((4, 4, 4, 8, w), BF16) for w in WIDTHS] * 3

    def shape(t, stage):
        s = [1, 1, 1]
        for k, a in enumerate(ORDERS[t]):
            if k < stage:
                s[AX[a]] = 4
        return tuple(s) + (8, WIDTHS[t])

    for stage in (2, 1, 0):
        out += [v((4,) + shape(t, stage), BF16) for t in range(3)]
    for stage in (2, 1):
        out += [v(shape(t, stage), F32) for t in range(3)]
    out += [v((4, 1024), BF16), v((4, 1024), BF16)]
    out += [
        dma(2, 16), dma(2, 16), dma(2, 16), dma(2, 8), dma(2, 8), dma(2),
        dma(2, 3, 3, 4), dma(2, 3, 9), dma(2, 3), dma(2, 3, 3, 4), dma(2),
    ]
    return out


def params(cid=None):
    if cid is None:
        return pltpu.CompilerParams(vmem_limit_bytes=LIMIT)
    return pltpu.CompilerParams(vmem_limit_bytes=LIMIT, collective_id=cid, has_side_effects=True)


def shards(
    hidden,
    queries,
    new_kv,
    kv_cache,
    block_table,
    seq_lens,
    w_uk,
    w_uv,
    o_proj,
    norm_gain,
    routes,
    gate_weights,
    w_gate,
    w_up,
    w_down,
    shared_gate,
    shared_up,
    shared_down,
):
    pages = kv_cache.shape[1]
    pool_rank = lax.axis_index("pool")
    sds = jax.ShapeDtypeStruct

    table = block_table[0] - pool_rank * pages
    lengths = seq_lens[0]
    req = lax.broadcasted_iota(jnp.int32, table.shape, 0)
    slot = lax.broadcasted_iota(jnp.int32, table.shape, 1)
    filled = jnp.clip(lengths[:, None] - slot * 128, 0, 128)
    hit = (table[None] == jnp.arange(pages, dtype=jnp.int32)[:, None, None]) & (filled > 0)[None]
    code = jnp.sum(jnp.where(hit, (req * 256 + filled)[None], 0), axis=(1, 2))
    own = jnp.arange(4, dtype=jnp.int32)
    meta = jnp.stack(
        [
            jnp.concatenate([code // 256, pool_rank * 4 + own]),
            jnp.concatenate([jnp.zeros((pages,), jnp.int32), own]),
            jnp.concatenate([code % 256, own + 1]),
        ]
    )
    fresh = jnp.pad(new_kv[0].T, ((0, 0), (0, 124)))
    experts = jnp.arange(64, dtype=jnp.int32)
    dense = jnp.sum(
        jnp.where(routes[0].reshape(32, 6)[:, :, None] == experts, gate_weights[0].reshape(32, 6)[:, :, None], 0.0),
        axis=1,
    )
    coarse = dense.astype(BF16)
    gates = jnp.concatenate([coarse, (dense - coarse.astype(F32)).astype(BF16)], axis=1)

    qg = pl.pallas_call(
        gather_queries,
        out_shape=sds((16, 4, 16, 192), BF16),
        in_specs=[VM],
        out_specs=VM,
        scratch_shapes=[dma(16), dma(16)],
        compiler_params=params(0),
        name="gather_queries",
    )(queries[0])
    v = pltpu.VMEM
    parts, stats = pl.pallas_call(
        attention,
        out_shape=(sds((16, 4, 2048), BF16), sds((16, 4, 128), F32)),
        in_specs=[SM, VM, VM, VM, HBM, VM],
        out_specs=(VM, VM),
        scratch_shapes=[
            v((49, 576, 128), BF16), v((2, 1024, 128), F32), v((5, 1024, 128), F32), v((52, 16, 128), F32),
            v((1024, 128), F32), v((1024, 128), F32), v((4, 1024, 128), F32), v((64, 2048), F32),
            v((64, 128), F32), dma(6),
        ],
        compiler_params=params(),
        name="attention",
    )(meta, qg.reshape(64, 16, 192), w_uk, w_uv, jnp.swapaxes(kv_cache[0], 1, 2), fresh)
    wide = lambda w: jnp.swapaxes(w, -1, -2)
    attn, layer = pl.pallas_call(
        rest,
        out_shape=(sds((4, 2048), BF16), sds((4, 2048), BF16)),
        in_specs=[VM] * 5 + [HBM] * 7,
        out_specs=(VM, VM),
        scratch_shapes=rest_scratch(),
        compiler_params=params(1),
        name="rest",
    )(
        parts, stats, hidden[0], norm_gain[None], gates, o_proj, wide(w_gate), wide(w_up), w_down,
        wide(shared_gate), wide(shared_up), shared_down,
    )
    return attn[None], layer[None]


def solution(mesh):
    placed = (
        P("rep", "pool", None),
        P("rep", "pool", None, None),
        P("rep", "pool", None),
        P("rep", "pool", None, None),
        P("rep", None, None),
        P("rep", None),
        P(),
        P(),
        P("rep", None),
        P(),
        P("pool", None, None, None),
        P("pool", None, None, None),
        P("pool", None, "rep"),
        P("pool", None, "rep"),
        P("pool", "rep", None),
        P(None, "rep"),
        P(None, "rep"),
        P("rep", None),
    )
    return jax.shard_map(
        shards,
        mesh=mesh,
        in_specs=placed,
        out_specs=(P("rep", "pool", None), P("rep", "pool", None)),
        check_vma=False,
    )
```

time: 537 us -> 110 us (0.20)
  local copies, waits for them, and re-layouts: 178 us -> 4.6 us
  waiting for transfers between devices: 171 us -> 0 us
  blocking collectives: 123 us -> 0 us
  Pallas kernels: 0 us -> 98.8 us
  matrix products: 29.7 us -> 0 us
  between operations: 15.5 us -> 0.74 us
    scatter x4 -> x0, local copies, waits for them, and re-layouts: 126 us -> none  [the longest x2 60.9 us: shards(): jnp.zeros((pages_local,), jnp.int32).at[target]]
    unnamed x6 -> x0, waiting for transfers between devices: 111 us -> none
    pallas_call x0 -> x3, Pallas kernels: none -> 98.8 us  [the longest x1 69.3 us: shards(): pl.pallas_call(rest, out_shape=(sds((4, 2048), BF16), sds((4, 2048), BF16...]
    reduce_scatter x1 -> x0, waiting for transfers between devices: 41.9 us -> none  [shards(): lax.psum_scatter(numerator.astype(jnp.bfloat16), 'pool', scatter_dimensio...]
    pmax x1 -> x0, blocking collectives: 35.9 us -> none  [shards(): peak_used = lax.pmax(local_peak, 'pool')]
    all_gather x2 -> x0, blocking collectives: 30.7 us -> none  [the longest x1 15.3 us: shards(): column_heads = lax.all_gather(head_values, 'rep', axis=0, tiled=True)]
    dot_general x12 -> x0, matrix products: 29.7 us -> none  [the longest x1 5.29 us: shards(): jnp.einsum('pecf,efd->pecd', inner_act, w_down, preferred_element_type=jn...]
    unnamed x1 -> x0, blocking collectives: 28.6 us -> none
  transfers between devices with their start and end apart: 5 -> 0, of which waited for: 4 -> 0; matrix products, arithmetic and copies ran while one was open for 21% -> 0% of each run, Pallas kernels for 0% -> 0%
where the time goes in v1:
time: 110 us; the launch traced here: 109 us
  Pallas kernels  98.8 us (90%)
  other arithmetic  5.35 us (5%)
  local copies, waits for them, and re-layouts  4.6 us (4%)
    pallas_call x1, Pallas kernels, shards(): pl.pallas_call(rest, out_shape=(sds((4, 2048), BF16), sds((4, 2048), BF16...  69.3 us
    pallas_call x1, Pallas kernels, shards(): pl.pallas_call(gather_queries, out_shape=sds((16, 4, 16, 192), BF16), in_...  16 us
    pallas_call x1, Pallas kernels, shards(): pl.pallas_call(attention, out_shape=(sds((16, 4, 2048), BF16), sds((16, 4...  13.5 us
    unnamed x9, local copies, waits for them, and re-layouts  3.76 us

profile of v1, /device:TPU:1, one launch (start us, length us, event | category | flops | bytes accessed | tf_op | source)
XLA Modules:
  0.0 109.5 jit_solution(5999123080055979132)
XLA Ops:
  0.6 0.7 fusion.1
  1.4 0.7 fusion.2
  2.1 0.8 subtract_bitcast_fusion
  2.9 1.0 select_reduce_fusion
  3.9 0.1 add_bitcast_fusion
  4.0 1.2 %pad_add_fusion.meta = s32[3,52]{1,0:T(4,128)} fusion(s32[1,52]{1,0:T(1,128)S(1)} %get-tuple-element.15, s32[1,52]{1,0:T(1,128)} %constant.50.clone.1, s32[1,52]{1,0:T(1,128)S(1)} %get-tuple-element.14), kind=kLoop, calls=%fused_computation.11 | loop fusion | flops 312 | bytes 1248 | tf_op jit(solution)/shard_map/stack | solution.py:525
  5.2 16.0 %gather_queries.1 = bf16[16,4,16,192]{3,2,1,0:T(8,128)(2,1)} custom-call(bf16[4,16,192]{2,1,0:T(8,128)(2,1)} %bitcast.38), custom_call_target="tpu_custom_call" | custom-call | tf_op jit(solution)/shard_map/gather_queries/pallas_call | solution.py:541
  21.2 0.9 copy.26
  22.1 0.7 pad.5.fresh
  22.8 0.0 copy-start
  22.8 0.0 copy-start.1
  22.8 13.5 %attention.1 = (bf16[16,4,2048]{2,1,0:T(4,128)(2,1)}, f32[16,4,128]{2,1,0:T(4,128)}) custom-call(s32[3,52]{1,0:T(4,128)} %pad_add_fusion.meta, bf16[64,16,192]{2,1,0:T(8,128)(2,1)} %bitcast.34, bf16[16,128,512]{2,1,0:T(8,128)(2,1)} %wuk.1, bf16[16,512,128]{2,1,0:T(8,128)(2,1)} %wuv.1, bf16[48,576,128]{2,1,0:T(8,128)(2,1)} %bitcast.31, bf16[576,128]{1,0:T(8,128)(2,1)} %pad.5.fresh), custom_call_target="tpu_custom_call" | custom-call | tf_op jit(solution)/shard_map/attention/pallas_call | solution.py:551
  36.3 0.0 copy-done
  36.3 0.1 copy.28
  36.4 0.1 broadcast_in_dim.44
  36.5 0.0 copy-done.1
  36.5 0.1 copy.27
  36.6 0.1 eq.36
  36.7 0.1 select_reduce_fusion.1
  36.8 0.7 pad_maximum_fusion.gates_in
  37.5 69.3 %rest.1 = (bf16[4,2048]{1,0:T(4,128)(2,1)}, bf16[4,2048]{1,0:T(4,128)(2,1)}) custom-call(bf16[16,4,2048]{2,1,0:T(4,128)(2,1)} %get-tuple-element.6.p_ref, f32[16,4,128]{2,1,0:T(4,128)} %get-tuple-element.7.st_ref, bf16[4,2048]{1,0:T(4,128)(2,1)} %bitcast.39, f32[1,2048]{1,0:T(1,128)} %bitcast.42, bf16[32,128]{1,0:T(8,128)(2,1)} %pad_maximum_fusion.gates_in, ...), custom_call_target="tpu_custom_call" | custom-call | tf_op jit(solution)/shard_map/rest/pallas_call | solution.py:565
  106.8 1.3 %copy.31 = bf16[1,4,2048]{2,1,0:T(4,128)(2,1)} copy(bf16[1,4,2048]{2,1,0:T(4,128)(2,1)} %bitcast.41) | data formatting | bytes 32768
  108.1 1.3 %copy.32 = bf16[1,4,2048]{2,1,0:T(4,128)(2,1)} copy(bf16[1,4,2048]{2,1,0:T(4,128)(2,1)} %bitcast.40) | data formatting | bytes 32768
  (6 shorter events, 0.0 us)
Async XLA Ops:
  22.8 13.5 %copy-start = (f32[1,8,4,6]{1,2,3,0:T(4,128)S(1)}, f32[1,8,4,6]{1,2,3,0:T(4,128)}, u32[]{:S(2)}) copy-start(f32[1,8,4,6]{1,2,3,0:T(4,128)} %param.29) | copy-start | bytes 2308
  22.8 13.7 %copy-start.1 = (s32[1,8,4,6]{1,2,3,0:T(4,128)S(1)}, s32[1,8,4,6]{1,2,3,0:T(4,128)}, u32[]{:S(2)}) copy-start(s32[1,8,4,6]{1,2,3,0:T(4,128)} %param.28) | copy-start | bytes 2308

commit v2 on v1

v2 whole, which is shorter than its diff:
```python
import functools

import jax
import jax.numpy as jnp
from jax import lax
from jax.experimental import pallas as pl
from jax.experimental.pallas import tpu as pltpu
from jax.sharding import PartitionSpec as P

F32 = jnp.float32
BF16 = jnp.bfloat16
NEG = -1e30
EPS = 1e-06
STOP = 99
NX = 4
MESH = pl.DeviceIdType.MESH
VM = pl.BlockSpec(memory_space=pltpu.VMEM)
HBM = pl.BlockSpec(memory_space=pl.ANY)
SM = pl.BlockSpec(memory_space=pltpu.SMEM)
NT = (((1,), (1,)), ((), ()))
LIMIT = 60 * 1024 * 1024


def dot(a, b):
    return jnp.dot(a, b, preferred_element_type=F32)


def dot_nt(a, b):
    return lax.dot_general(a, b, NT, preferred_element_type=F32)


def place():
    p = lax.axis_index("pool")
    r = lax.axis_index("rep")
    return p // NX, p % NX, r // 2, r % 2


def pool_peers(x, z):
    out = []
    for d in range(1, 16):
        dx, dz = d // 4, d % 4
        out.append((d, ((x + dx) % 4) * 4 + (z + dz) % 4))
    return out


def rep_peers(y, c):
    out = []
    for d in range(1, 8):
        dy, dc = d // 2, d % 2
        out.append((d, ((y + dy) % 4) * 2 + (c + dc) % 2))
    return out


def send(src, dst, ssem, rsem, pool=None, rep=None):
    dev = {}
    if pool is not None:
        dev["pool"] = pool
    if rep is not None:
        dev["rep"] = rep
    cp = pltpu.make_async_remote_copy(
        src_ref=src, dst_ref=dst, send_sem=ssem, recv_sem=rsem, device_id=dev, device_id_type=MESH
    )
    cp.start()
    return cp


def greet(devices):
    bar = pltpu.get_barrier_semaphore()
    for dev in devices:
        pl.semaphore_signal(bar, inc=1, device_id=dev, device_id_type=MESH)
    pl.semaphore_wait(bar, len(devices))


WIDTHS = (384, 384, 256)
STARTS = (0, 384, 768)
ORDERS = (("x", "z", "y"), ("z", "y", "x"), ("y", "x", "z"))
STEPS = (0, 1, 3, 2)
AX = {"x": 0, "z": 1, "y": 2}


def layer(
    q_in, table_in, len_in, new_in, hid, gain, gates_in,
    wuk_h, wuv_h, cache, oproj_h, wg_h, wu_h, wd_h, sg_h, su_h, sd_h,
    proj_out, moe_out,
    wuk, wuv, kv, oproj, wg, wu, wd, sg, su, sd, wsem, kvsem,
    qp, qg, qf, qr, fq, nb, mb, db, mrow, meta_v, wide, vb, of, sf, pbuf, stbuf, qsem,
    rp, rst, gates, heads, hs, hb, hbf, pf, ps, pr, nown, npart, blk,
    x0, x1, x2, xm, inner, shin, y0, y1, y2, cs0, cs1, cs2, cr0, cr1, cr2,
    sb0, sb1, sb2, ra0, ra1, ra2, rb0, rb1, rb2, fs, fr,
    psem, ssem, gsem, hsem, osem, nsem, asem, bsem, fsem, csem, dsem, esem, lsem,
):
    x, z, y, c = place()
    me = x * 4 + z
    rp_me = y * 2 + c
    coord = {"x": x, "z": z, "y": y}
    pools = pool_peers(x, z)
    reps = rep_peers(y, c)
    mate = y * 2 + 1 - c
    xs = (x0, x1, x2)
    pages, chunk, rows = 48, 8, 64
    scale = 192 ** (-0.5)

    def load(h, v, sem):
        cp = pltpu.make_async_copy(h, v, sem)
        cp.start()
        return cp

    wl = {0: load(wuk_h, wuk, wsem.at[0])}
    kl = []
    for i in range(pages // chunk):
        s = pl.ds(i * chunk, chunk)
        kl.append(load(cache.at[s], kv.at[s], kvsem.at[i]))
    def peer(**over):
        at = {a: (coord[a] + over.get(a, 0)) % 4 for a in "xzy"}
        return {"pool": at["x"] * 4 + at["z"], "rep": at["y"] * 2 + c}

    def more():
        for i, (h, v) in enumerate(
            ((wuv_h, wuv), (oproj_h, oproj), (sg_h, sg), (su_h, su), (sd_h, sd), (wg_h, wg), (wu_h, wu), (wd_h, wd))
        ):
            wl[i + 1] = load(h, v, wsem.at[i + 1])

    def bail(*waits):
        for cp in waits:
            cp.wait()
        proj_out[...] = jnp.zeros((4, 2048), F32)
        moe_out[...] = jnp.zeros((4, 2048), F32)

    for k in range(4):
        v = q_in[k].astype(F32)
        qp[k, 0:16, :] = v[:, 0:128].astype(BF16)
        qp[k, 16:24, :] = jnp.concatenate([v[0:8, 128:192], v[8:16, 128:192]], axis=1).astype(BF16)
    greet(
        [{"pool": q, "rep": rp_me} for _, q in pools]
        + [{"pool": me, "rep": q} for _, q in reps]
        + [peer(**{a: da, "y": dy}) for a in "xz" for da in range(1, 4) for dy in range(1, 4)]
    )
    if STOP == 0:
        return bail(*wl.values(), *kl)

    first = [send(qp, qg.at[x, z], qsem.at[0, d], qsem.at[1, d], pool=q) for d, q in pools]
    qg[x, z] = qp[...]

    sub = lax.broadcasted_iota(jnp.int32, (64, 128), 0)
    lane = lax.broadcasted_iota(jnp.int32, (64, 128), 1)
    lens = jnp.broadcast_to(len_in[...], (64, 64))
    diag = lax.broadcasted_iota(jnp.int32, (64, 64), 0) == lax.broadcasted_iota(jnp.int32, (64, 64), 1)
    lens = jnp.sum(jnp.where(diag, lens, 0), axis=1, keepdims=True)
    filled = jnp.clip(lens - lane * 128, 0, 128)
    code = sub * 256 + filled
    local = jnp.where(filled > 0, table_in[...] - me * pages, -1)
    for i in range(pages):
        mrow[i : i + 1, :] = jnp.sum(jnp.where(local == i, code, 0), axis=0, keepdims=True)
    mrow[pages:rows, :] = jnp.zeros((rows - pages, 128), jnp.int32)
    codes = jnp.broadcast_to(jnp.sum(mrow[...], axis=1, keepdims=True), (rows, 128))
    meta_v[...] = codes % 256
    virtual = (sub >= pages) & (sub < pages + 4)
    owner = jnp.where(virtual, me * 4 + sub - pages, codes // 256)

    wide[...] = jnp.zeros((128, 640), F32)
    wide[0:4, 0:576] = new_in[...].astype(F32)
    for t in range(5):
        n = 64 if t == 4 else 128
        kv[pages, t * 128 : t * 128 + n, :] = wide[:, t * 128 : (t + 1) * 128].T[0:n, :].astype(BF16)
    mb[pages * 16 + 64 :, :] = jnp.full(((rows - pages - 4) * 16, 128), NEG, F32)
    db[pages * 16 + 64 :, :] = jnp.zeros(((rows - pages - 4) * 16, 128), F32)
    for t in range(4):
        nb[t, pages * 16 + 64 :, :] = jnp.zeros(((rows - pages - 4) * 16, 128), F32)

    for cp in first:
        cp.wait()
    gc = [send(gates_in, gates.at[me], gsem.at[0, d], gsem.at[1, d], pool=q) for d, q in pools]
    gates[me] = gates_in[...]
    more()
    wl[0].wait()
    if STOP == 1:
        return bail(*[wl[i] for i in range(1, 9)], *kl, *gc)

    @pl.loop(0, 64, unroll=4)
    def _(j):
        v = qg[j // 16, (j // 4) % 4, j % 4].astype(F32)
        qf[pl.ds(pl.multiple_of(j * 16, 16), 16), :] = v[0:16]
        qr[pl.ds(pl.multiple_of(j * 8, 8), 8), :] = v[16:24]

    hot = jnp.where(lane == owner, 1.0, 0.0)
    pick = hot[:, 0:64].astype(BF16)
    for h in range(16):
        s = pl.ds(h, 64, stride=16)
        a = dot(dot(pick, qf[s, :].astype(BF16)).astype(BF16), wuk[h]) * scale
        for t in range(4):
            fq[t, s, :] = a[:, t * 128 : (t + 1) * 128]
        b = dot(pick, qr[pl.ds(h % 8, 64, stride=8), :].astype(BF16)) * scale
        if h >= 8:
            b = jnp.concatenate([b[:, 64:128], b[:, 0:64]], axis=1)
        fq[4, s, :] = b
    if STOP == 2:
        return bail(*[wl[i] for i in range(1, 9)], *kl, *gc)
    lane16 = lax.broadcasted_iota(jnp.int32, (16, 128), 1)

    def page(i, ik, lo, hi):
        s = pl.ds(pl.multiple_of(i * 16, 16), 16)
        qa = jnp.concatenate([fq[t, s, :] for t in range(4)], axis=1).astype(BF16)
        qb = fq[4, s, :][:, 0:64].astype(BF16)
        v = dot(qa, kv[ik, 0:512, :]) + dot(qb, kv[ik, 512:576, :])
        ok = (lane16 >= lo) & (lane16 < hi)
        v = jnp.where(ok, v, NEG)
        m = jnp.max(v, axis=1, keepdims=True)
        w = jnp.where(ok, jnp.exp(v - m), 0.0).astype(BF16)
        den = jnp.sum(w.astype(F32), axis=1, keepdims=True)
        num = dot_nt(w, kv[ik, 0:512, :])
        o = pl.ds(pl.multiple_of(i * 16, 16), 16)
        mb[o, :] = jnp.broadcast_to(m, (16, 128))
        db[o, :] = jnp.broadcast_to(den, (16, 128))
        for t in range(4):
            nb[t, o, :] = num[:, t * 128 : (t + 1) * 128]

    for k in range(4):
        page(pages + k, pages, k, k + 1)
    for cp in kl:
        cp.wait()

    @pl.loop(0, pages // 8)
    def _(g):
        for u in range(8):
            i = g * 8 + u
            page(i, i, 0, meta_v[pl.ds(i, 1), :])

    if STOP == 3:
        return bail(*[wl[i] for i in range(1, 9)], *gc)

    m = jnp.full((rows, 128), NEG, F32)
    d = jnp.zeros((rows, 128), F32)
    for h in range(16):
        s = pl.ds(h, rows, stride=16)
        m = jnp.where(lane == h, mb[s, :], m)
        d = jnp.where(lane == h, db[s, :], d)
    sf[...] = m
    meta_v[...] = owner
    lp = jnp.full((rows, 128), NEG, F32)
    lr = lp
    for i in range(pages + 4):
        o = meta_v[i : i + 1, :]
        row = sf[i : i + 1, :]
        lp = jnp.maximum(lp, jnp.where(owner == o, row, NEG))
        lr = jnp.maximum(lr, jnp.where(sub == o, row, NEG))
    e = jnp.exp(m - lp)
    hot = hot.T[0:64, :]
    rd = lax.dot_general(
        hot, e * d, (((1,), (0,)), ((), ())), preferred_element_type=F32, precision=lax.Precision.HIGHEST
    )
    wl[1].wait()
    for h in range(16):
        s = pl.ds(h, rows, stride=16)
        a = jnp.concatenate([nb[t, s, :] for t in range(4)], axis=1).astype(BF16)
        vb[:, h * 128 : (h + 1) * 128] = (dot(a, wuv[h]) * e[:, h : h + 1]).astype(BF16)
    full = rd > 0.0
    safe = jnp.where(full, rd, 1.0)
    inv = 1.0 / safe
    sf[...] = jnp.where(full, lr + jnp.log(safe), NEG)
    hot = hot.astype(BF16)
    for h in range(0, 16, 4):
        v = dot(hot, vb[:, h * 128 : (h + 4) * 128])
        for u in range(4):
            of[:, (h + u) * 128 : (h + u + 1) * 128] = v[:, u * 128 : (u + 1) * 128] * inv[:, h + u : h + u + 1]
    for k in range(16):
        pbuf[k] = of[k * 4 : (k + 1) * 4, :].astype(BF16)
        stbuf[k] = sf[k * 4 : (k + 1) * 4, :]
    if STOP == 4:
        return bail(*[wl[i] for i in range(2, 9)], *gc)
    sc = [send(stbuf.at[q], rst.at[me], ssem.at[0, d], ssem.at[1, d], pool=q) for d, q in pools]
    pc = [send(pbuf.at[q], rp.at[me], psem.at[0, d], psem.at[1, d], pool=q) for d, q in pools]
    rst[me] = stbuf[me]
    rp[me] = pbuf[me]
    for cp in sc:
        cp.wait()
    top = rst[0]
    for s in range(1, 16):
        top = jnp.maximum(top, rst[s])
    tot = jnp.zeros((4, 128), F32)
    for s in range(16):
        e = jnp.exp(rst[s] - top)
        rst[s] = e
        tot = tot + e
    inv = 1.0 / tot
    for cp in pc:
        cp.wait()

    heads[...] = jnp.zeros((4, 2048), F32)

    @pl.loop(0, 16)
    def _(s):
        w = rst[s] * inv
        for h in range(16):
            cols = slice(h * 128, (h + 1) * 128)
            heads[:, cols] = heads[:, cols] + w[:, h : h + 1] * rp[s, :, cols].astype(F32)

    if STOP == 5:
        return bail(*[wl[i] for i in range(2, 9)], *gc)
    for g in range(8):
        hs[g] = heads[:, g * 256 : (g + 1) * 256].astype(BF16)
    hc = [send(hs.at[q], hb.at[rp_me], hsem.at[0, d], hsem.at[1, d], rep=q) for d, q in reps]
    hb[rp_me] = hs[rp_me]
    wl[2].wait()
    for cp in hc:
        cp.wait()
    if STOP == 6:
        return bail(*[wl[i] for i in range(3, 9)], *gc)
    for g in range(8):
        hbf[g * 4 : (g + 1) * 4, :] = hb[g].astype(F32)
    pf[...] = dot(hbf[...].astype(BF16), oproj[...])
    for g in range(8):
        ps[g] = pf[g * 4 : (g + 1) * 4, :].astype(BF16)
    oc = [send(ps.at[q], pr.at[rp_me], osem.at[0, d], osem.at[1, d], rep=q) for d, q in reps]
    pr[rp_me] = ps[rp_me]
    for cp in oc:
        cp.wait()
    proj = pr[0].astype(F32)
    for g in range(1, 8):
        proj = proj + pr[g].astype(F32)
    proj_out[...] = proj
    res = hid[...].astype(F32) + proj
    ms = jnp.mean(res * res, axis=1, keepdims=True)
    normed = (res * lax.rsqrt(ms + EPS) * gain[...]).astype(BF16)

    if STOP == 7:
        return bail(*[wl[i] for i in range(3, 9)], *gc)
    nown[...] = normed
    cp = send(nown, npart, nsem.at[0], nsem.at[1], rep=mate)
    for g in gc:
        g.wait()
    cp.wait()
    mine = normed.astype(F32)
    theirs = npart[...].astype(F32)
    blk[0:4, :] = jnp.where(c == 0, mine, theirs)
    blk[4:8, :] = jnp.where(c == 0, theirs, mine)
    for t in range(3):
        s = pl.ds(pl.multiple_of(c * 1024 + STARTS[t], 128), WIDTHS[t])
        xs[t][c, x, z, y] = blk[:, s].astype(BF16)

    if STOP == 8:
        return bail(*[wl[i] for i in range(3, 9)])
    whole = pl.ds(0, 4)

    def idx(at):
        return tuple(at[a] if not isinstance(at[a], jax.Array) else pl.ds(at[a], 1) for a in "xzy")

    def near(a, d):
        return (coord[a] + d) % 4

    fwd = []

    def share(t, k, at):
        ref = xs[t].at[(c,) + idx(at)]
        fwd.append(send(ref, ref, fsem.at[0, t, k], fsem.at[1, t, k], rep=mate))

    flat = {}
    for da in STEPS:
        for db in STEPS:
            if da or db:
                for t in range(3):
                    a, b, _ = ORDERS[t]
                    ref = xs[t].at[(c,) + idx(coord)]
                    k = da * 4 + db
                    flat[t, k] = send(
                        ref, ref, asem.at[0, t, k], asem.at[1, t, k], **peer(**{a: da, b: db})
                    )
    last = {}
    for da in STEPS:
        for t in range(3):
            a, b, w = ORDERS[t]
            for db in range(4):
                if da or db:
                    flat[t, da * 4 + db].wait()
            at = {a: near(a, -da), b: whole, w: coord[w]}
            ref = xs[t].at[(c,) + idx(at)]
            for d in range(1, 4):
                k = da * 4 + d
                last[t, da, d] = send(ref, ref, bsem.at[0, t, k], bsem.at[1, t, k], **peer(**{w: d}))
    for t in range(3):
        a, b, w = ORDERS[t]
        share(t, 0, {a: whole, b: whole, w: coord[w]})
    for d in (1, 3, 2):
        for t in range(3):
            a, b, w = ORDERS[t]
            for da in STEPS:
                last[t, da, d].wait()
            share(t, d, {a: whole, b: whole, w: near(w, -d)})
    for cp in fwd:
        cp.wait()
    if STOP == 9:
        return bail(*[wl[i] for i in range(3, 9)])

    for t in range(3):
        for h in range(2):
            s = h * 1024 + STARTS[t]
            v = xs[t][h].astype(F32).reshape(512, WIDTHS[t]).astype(BF16)
            xm[:, s : s + WIDTHS[t]] = v

    for i in range(3, 9):
        wl[i].wait()

    col = xm[pl.ds(pl.multiple_of(me * 32, 32), 32), :]
    ga = dot_nt(col, sg[...])
    ua = dot_nt(col, su[...])
    shin[...] = (ga / (1.0 + jnp.exp(-ga)) * ua).astype(BF16)

    gm = gates[...].reshape(512, 128)
    ids = lax.broadcasted_iota(jnp.int32, (128, 176), 0) % 64

    @pl.loop(0, 4)
    def _(e):
        ga = dot_nt(xm[...], wg[e])
        ua = dot_nt(xm[...], wu[e])
        gw = dot(gm, jnp.where(ids == me * 4 + e, 1.0, 0.0).astype(BF16))
        inner[e] = (ga / (1.0 + jnp.exp(-ga)) * ua * gw).astype(BF16)

    if STOP == 10:
        return bail()
    ys = (y0, y1, y2)
    css = (cs0, cs1, cs2)
    crs = (cr0, cr1, cr2)
    cc = []

    def down(t, half):
        wdt = WIDTHS[t]
        cols = pl.ds(pl.multiple_of(half * 1024 + STARTS[t], 128), wdt)
        v = dot(inner[0], wd[0, :, cols])
        for e in range(1, 4):
            v = v + dot(inner[e], wd[e, :, cols])
        sh = dot(shin[...], sd[:, cols])
        ys[t][...] = v.reshape(4, 4, 4, 8, wdt)
        ys[t][x, z] = ys[t][x, z] + sh.reshape(4, 8, wdt)

    for t in range(3):
        down(t, 1 - c)
        css[t][...] = ys[t][...].astype(BF16)
        cc.append(send(css[t], crs[t], csem.at[0, t], csem.at[1, t], rep=mate))

    sbs = (sb0, sb1, sb2)
    ras, rbs = (ra0, ra1, ra2), (rb0, rb1, rb2)

    back = (2, 1, 3, 0)
    away = {}
    for t in range(3):
        down(t, c)
        cc[t].wait()
        tot = ys[t][...] + crs[t][...].astype(F32)
        ys[t][...] = tot
        sbs[t][...] = tot.astype(BF16)
        a, b, w = ORDERS[t]
        for da in back:
            for d in range(1, 4):
                src = sbs[t].at[idx({a: near(a, da), b: whole, w: near(w, d)})]
                dst = ras[t].at[(d,) + idx({a: near(a, da), b: whole, w: coord[w] * 0})]
                k = da * 4 + d
                away[t, da, d] = send(src, dst, dsem.at[0, t, k], dsem.at[1, t, k], **peer(**{w: d}))
    if STOP == 11:
        return bail(*away.values())
    home = {}
    own = {}
    for da in back:
        for t in range(3):
            a, b, w = ORDERS[t]
            for d in range(1, 4):
                away[t, da, d].wait()
            at = idx({a: near(a, da), b: whole, w: coord[w] * 0})
            v = ys[t][idx({a: near(a, da), b: whole, w: coord[w]})]
            for d in range(1, 4):
                v = v + ras[t][(d,) + at].astype(F32)
            ras[t][(0,) + at] = v.astype(BF16)
            for db in back:
                k = da * 4 + db
                if k:
                    ref = ras[t].at[(0,) + idx({a: near(a, da), b: near(b, db), w: coord[w] * 0})]
                    dst = rbs[t].at[(k,) + (pl.ds(0, 1),) * 3]
                    home[t, k] = send(ref, dst, esem.at[0, t, k], esem.at[1, t, k], **peer(**{a: da, b: db}))
    for t in range(3):
        a, b, w = ORDERS[t]
        v = ras[t][(0,) + idx({a: coord[a], b: coord[b], w: coord[w] * 0})].astype(F32)
        for k in range(1, 16):
            home[t, k].wait()
            v = v + rbs[t][k].astype(F32)
        blk[:, STARTS[t] : STARTS[t] + WIDTHS[t]] = v.reshape(8, WIDTHS[t])
    lo, hi = blk[0:4, 0:1024], blk[4:8, 0:1024]
    fs[...] = jnp.where(c == 0, hi, lo).astype(BF16)
    cp = send(fs, fr, lsem.at[0], lsem.at[1], rep=mate)
    own = jnp.where(c == 0, lo, hi)
    cp.wait()
    other = fr[...].astype(F32)
    moe_out[:, 0:1024] = jnp.where(c == 0, own, other)
    moe_out[:, 1024:2048] = jnp.where(c == 0, other, own)


def dma(*shape):
    return pltpu.SemaphoreType.DMA(shape)


def scratch():
    v = pltpu.VMEM
    i32 = jnp.int32
    big = [v((4, 176, 2048), BF16)] * 3 + [v((352, 2048), BF16)] * 3
    out = [v((16, 128, 512), BF16), v((16, 512, 128), BF16), v((49, 576, 128), BF16), v((256, 2048), BF16)]
    out += big + [dma(9), dma(6)]
    out += [
        v((4, 24, 128), BF16), v((4, 4, 4, 24, 128), BF16), v((1024, 128), F32), v((512, 128), F32),
        v((5, 1024, 128), F32), v((4, 1024, 128), F32), v((1024, 128), F32), v((1024, 128), F32),
        v((64, 128), i32), v((64, 128), i32), v((128, 640), F32),
        v((64, 2048), BF16), v((64, 2048), F32), v((64, 128), F32), v((16, 4, 2048), BF16),
        v((16, 4, 128), F32), dma(2, 16),
    ]
    out += [
        v((16, 4, 2048), BF16), v((16, 4, 128), F32), v((16, 32, 128), BF16), v((4, 2048), F32),
        v((8, 4, 256), BF16), v((8, 4, 256), BF16), v((32, 256), F32), v((32, 2048), F32),
        v((8, 4, 2048), BF16), v((8, 4, 2048), BF16), v((4, 2048), BF16), v((4, 2048), BF16),
        v((8, 2048), F32),
    ]
    out += [v((2, 4, 4, 4, 8, w), BF16) for w in WIDTHS]
    out += [v((512, 2048), BF16), v((4, 512, 176), BF16), v((32, 352), BF16)]
    out += [v((4, 4, 4, 8, w), F32) for w in WIDTHS]
    out += [v((4, 4, 4, 8, w), BF16) for w in WIDTHS] * 3

    def shape(t):
        return tuple(1 if a == ORDERS[t][2] else 4 for a in "xzy") + (8, WIDTHS[t])

    out += [v((4,) + shape(t), BF16) for t in range(3)]
    out += [v((16, 1, 1, 1, 8, w), BF16) for w in WIDTHS]
    out += [v((4, 1024), BF16), v((4, 1024), BF16)]
    out += [
        dma(2, 16), dma(2, 16), dma(2, 16), dma(2, 8), dma(2, 8), dma(2),
        dma(2, 3, 16), dma(2, 3, 16), dma(2, 3, 4), dma(2, 3), dma(2, 3, 16), dma(2, 3, 16), dma(2),
    ]
    return out


def params(cid):
    return pltpu.CompilerParams(vmem_limit_bytes=LIMIT, collective_id=cid, has_side_effects=True)


def call(q, table, lens, new, hid, gain, gates, *weights):
    sds = jax.ShapeDtypeStruct
    return pl.pallas_call(
        layer,
        out_shape=(sds((4, 2048), F32), sds((4, 2048), F32)),
        in_specs=[VM] * 7 + [HBM] * 10,
        out_specs=(VM, VM),
        scratch_shapes=scratch(),
        compiler_params=params(0),
        name="layer",
    )(q, table, lens, new, hid, gain, gates, *weights)


def shards(
    hidden,
    queries,
    new_kv,
    kv_cache,
    block_table,
    seq_lens,
    w_uk,
    w_uv,
    o_proj,
    norm_gain,
    routes,
    gate_weights,
    w_gate,
    w_up,
    w_down,
    shared_gate,
    shared_up,
    shared_down,
):
    experts = jnp.arange(64, dtype=jnp.int32)
    dense = jnp.sum(
        jnp.where(routes[0].reshape(32, 6)[:, :, None] == experts, gate_weights[0].reshape(32, 6)[:, :, None], 0.0),
        axis=1,
    )
    coarse = dense.astype(BF16)
    gates = jnp.concatenate([coarse, (dense - coarse.astype(F32)).astype(BF16)], axis=1)

    wide = lambda w: jnp.swapaxes(w, -1, -2)
    proj, moe = call(
        queries[0], block_table[0], seq_lens, new_kv[0], hidden[0], norm_gain[None], gates,
        w_uk, w_uv, wide(kv_cache[0]), o_proj, wide(w_gate), wide(w_up), w_down,
        wide(shared_gate), wide(shared_up), shared_down,
    )
    layer_out = (hidden[0].astype(F32) + proj + moe).astype(BF16)
    return proj.astype(BF16)[None], layer_out[None]


def solution(mesh):
    placed = (
        P("rep", "pool", None),
        P("rep", "pool", None, None),
        P("rep", "pool", None),
        P("rep", "pool", None, None),
        P("rep", None, None),
        P("rep", None),
        P(),
        P(),
        P("rep", None),
        P(),
        P("pool", None, None, None),
        P("pool", None, None, None),
        P("pool", None, "rep"),
        P("pool", None, "rep"),
        P("pool", "rep", None),
        P(None, "rep"),
        P(None, "rep"),
        P("rep", None),
    )
    return jax.shard_map(
        shards,
        mesh=mesh,
        in_specs=placed,
        out_specs=(P("rep", "pool", None), P("rep", "pool", None)),
        check_vma=False,
    )
```

time: 110 us -> 99.3 us (0.903)
  Pallas kernels: 98.8 us -> 94.3 us
  other arithmetic: 5.35 us -> 2.27 us
  local copies, waits for them, and re-layouts: 4.6 us -> 1.78 us
    pallas_call x3 -> x1, Pallas kernels: 98.8 us -> 94.3 us  [call(): pl.pallas_call(layer, out_shape=(sds((4, 2048), F32), sds((4, 2048), F32)...]
    unnamed x9 -> x4, local copies, waits for them, and re-layouts: 3.76 us -> 1.63 us
    broadcast_in_dim x0 -> x1, other arithmetic: none -> 1.46 us  [shards(): return (proj.astype(BF16)[None], layer_out[None])]
    another operation x2 -> x0, other arithmetic: 1.32 us -> none  [shards(): jnp.stack([jnp.concatenate([code // 256, pool_rank * 4 + own]), jnp.conca...]
where the time goes in v2:
time: 99.3 us; the launch traced here: 99 us
  Pallas kernels  94.3 us (95%)
  other arithmetic  2.27 us (2%)
  local copies, waits for them, and re-layouts  1.78 us (2%)
    pallas_call x1, Pallas kernels, call(): pl.pallas_call(layer, out_shape=(sds((4, 2048), F32), sds((4, 2048), F32)...  94.3 us

profile of v2, /device:TPU:1, one launch (start us, length us, event | category | flops | bytes accessed | tf_op | source)
XLA Modules:
  0.0 99.0 jit_solution(676081503397682473)
XLA Ops:
  0.6 0.8 copy.24
  1.4 0.1 eq.15
  1.5 0.8 copy.25
  2.3 0.1 broadcast_in_dim.25
  2.4 0.1 select_reduce_fusion
  2.5 0.7 pad_maximum_fusion.gates_in
  3.2 0.0 copy-start
  3.2 94.3 %layer.1 = (f32[4,2048]{1,0:T(4,128)}, f32[4,2048]{1,0:T(4,128)}) custom-call(bf16[4,16,192]{2,1,0:T(8,128)(2,1)} %bitcast.31, s32[64,128]{1,0:T(8,128)} %bitcast.32, s32[1,64]{1,0:T(1,128)} %len_in.1, bf16[4,576]{1,0:T(4,128)(2,1)} %bitcast.34, bf16[4,2048]{1,0:T(4,128)(2,1)} %bitcast.30, f32[1,2048]{1,0:T(1,128)} %bitcast.33, ...), custom_call_target="tpu_custom_call" | custom-call | tf_op jit(solution)/shard_map/layer/pallas_call | solution.py:541
  97.5 0.0 copy-done
  97.5 1.5 %fusion = (bf16[1,4,2048]{2,1,0:T(4,128)(2,1)}, bf16[1,4,2048]{2,1,0:T(4,128)(2,1)}) fusion(f32[4,2048]{1,0:T(4,128)} %get-tuple-element.5, f32[4,2048]{1,0:T(4,128)} %get-tuple-element.4, bf16[1,4,2048]{2,1,0:T(4,128)(2,1)S(1)} %copy-done), kind=kLoop, calls=%fused_computation.3 | loop fusion | flops 40960 | bytes 114688 | tf_op jit(solution)/shard_map/broadcast_in_dim | solution.py:587
  (1 shorter events, 0.0 us)
Async XLA Ops:
  3.2 94.3 %copy-start = (bf16[1,4,2048]{2,1,0:T(4,128)(2,1)S(1)}, bf16[1,4,2048]{2,1,0:T(4,128)(2,1)}, u32[]{:S(2)}) copy-start(bf16[1,4,2048]{2,1,0:T(4,128)(2,1)} %param.18) | copy-start | bytes 49156

commit v3 on v2

--- a/solution.py
+++ b/solution.py
@@ -64,11 +64,14 @@
     return cp
 
 
-def greet(devices):
+def hail(devices):
     bar = pltpu.get_barrier_semaphore()
     for dev in devices:
         pl.semaphore_signal(bar, inc=1, device_id=dev, device_id_type=MESH)
-    pl.semaphore_wait(bar, len(devices))
+
+
+def meet(devices):
+    pl.semaphore_wait(pltpu.get_barrier_semaphore(), len(devices))
 
 
 WIDTHS = (384, 384, 256)
@@ -79,12 +82,12 @@
 
 
 def layer(
-    q_in, table_in, len_in, new_in, hid, gain, gates_in,
+    q_in, table_in, len_in, new_in, hid, gain, routes_in, weights_in,
     wuk_h, wuv_h, cache, oproj_h, wg_h, wu_h, wd_h, sg_h, su_h, sd_h,
     proj_out, moe_out,
     wuk, wuv, kv, oproj, wg, wu, wd, sg, su, sd, wsem, kvsem,
     qp, qg, qf, qr, fq, nb, mb, db, mrow, meta_v, wide, vb, of, sf, pbuf, stbuf, qsem,
-    rp, rst, gates, heads, hs, hb, hbf, pf, ps, pr, nown, npart, blk,
+    rp, rst, gates_own, gates, heads, hs, hb, hbf, pf, ps, pr, nown, npart, blk,
     x0, x1, x2, xm, inner, shin, y0, y1, y2, cs0, cs1, cs2, cr0, cr1, cr2,
     sb0, sb1, sb2, ra0, ra1, ra2, rb0, rb1, rb2, fs, fr,
     psem, ssem, gsem, hsem, osem, nsem, asem, bsem, fsem, csem, dsem, esem, lsem,
@@ -126,21 +129,16 @@
         proj_out[...] = jnp.zeros((4, 2048), F32)
         moe_out[...] = jnp.zeros((4, 2048), F32)
 
+    known = (
+        [{"pool": q, "rep": rp_me} for _, q in pools]
+        + [{"pool": me, "rep": q} for _, q in reps]
+        + [peer(**{a: da, "y": dy}) for a in "xz" for da in range(1, 4) for dy in range(1, 4)]
+    )
+    hail(known)
     for k in range(4):
         v = q_in[k].astype(F32)
         qp[k, 0:16, :] = v[:, 0:128].astype(BF16)
         qp[k, 16:24, :] = jnp.concatenate([v[0:8, 128:192], v[8:16, 128:192]], axis=1).astype(BF16)
-    greet(
-        [{"pool": q, "rep": rp_me} for _, q in pools]
-        + [{"pool": me, "rep": q} for _, q in reps]
-        + [peer(**{a: da, "y": dy}) for a in "xz" for da in range(1, 4) for dy in range(1, 4)]
-    )
-    if STOP == 0:
-        return bail(*wl.values(), *kl)
-
-    first = [send(qp, qg.at[x, z], qsem.at[0, d], qsem.at[1, d], pool=q) for d, q in pools]
-    qg[x, z] = qp[...]
-
     sub = lax.broadcasted_iota(jnp.int32, (64, 128), 0)
     lane = lax.broadcasted_iota(jnp.int32, (64, 128), 1)
     lens = jnp.broadcast_to(len_in[...], (64, 64))
@@ -157,6 +155,31 @@
     virtual = (sub >= pages) & (sub < pages + 4)
     owner = jnp.where(virtual, me * 4 + sub - pages, codes // 256)
 
+    ids64 = lax.broadcasted_iota(jnp.int32, (64, 8), 0)
+    row32 = lax.broadcasted_iota(jnp.int32, (32, 8), 0)
+    col8 = lax.broadcasted_iota(jnp.int32, (32, 8), 1)
+    coarse = jnp.zeros((32, 64), F32)
+    fine = coarse
+    for q in range(4):
+        v = jnp.zeros((64, 8), F32)
+        for k in range(6):
+            v = v + jnp.where(routes_in[k, q : q + 1, :] == ids64, weights_in[k, q : q + 1, :], 0.0)
+        high = v.astype(BF16)
+        low = (v - high.astype(F32)).astype(BF16)
+        at = jnp.where(row32 == col8 * 4 + q, 1.0, 0.0).astype(BF16)
+        coarse = coarse + dot_nt(at, high)
+        fine = fine + dot_nt(at, low)
+    gates_own[...] = jnp.concatenate([coarse, fine], axis=1).astype(BF16)
+
+    meet(known)
+    if STOP == 0:
+        return bail(*wl.values(), *kl)
+
+    first = [send(qp, qg.at[x, z], qsem.at[0, d], qsem.at[1, d], pool=q) for d, q in pools]
+    qg[x, z] = qp[...]
+    if STOP == 20:
+        return bail(*wl.values(), *kl, *first)
+
     wide[...] = jnp.zeros((128, 640), F32)
     wide[0:4, 0:576] = new_in[...].astype(F32)
     for t in range(5):
@@ -169,12 +192,11 @@
 
     for cp in first:
         cp.wait()
-    gc = [send(gates_in, gates.at[me], gsem.at[0, d], gsem.at[1, d], pool=q) for d, q in pools]
-    gates[me] = gates_in[...]
-    more()
+    gc = [send(gates_own, gates.at[me], gsem.at[0, d], gsem.at[1, d], pool=q) for d, q in pools]
+    gates[me] = gates_own[...]
     wl[0].wait()
     if STOP == 1:
-        return bail(*[wl[i] for i in range(1, 9)], *kl, *gc)
+        return bail(*kl, *gc)
 
     @pl.loop(0, 64, unroll=4)
     def _(j):
@@ -194,36 +216,40 @@
             b = jnp.concatenate([b[:, 64:128], b[:, 0:64]], axis=1)
         fq[4, s, :] = b
     if STOP == 2:
-        return bail(*[wl[i] for i in range(1, 9)], *kl, *gc)
-    lane16 = lax.broadcasted_iota(jnp.int32, (16, 128), 1)
-
-    def page(i, ik, lo, hi):
-        s = pl.ds(pl.multiple_of(i * 16, 16), 16)
+        return bail(*kl, *gc)
+    more()
+    group = lax.broadcasted_iota(jnp.int32, (32, 256), 0) // 16
+    spot = lax.broadcasted_iota(jnp.int32, (32, 256), 1) - group * 128
+
+    def pair(i, one, two, lo, hi):
+        s = pl.ds(pl.multiple_of(i * 16, 32), 32)
         qa = jnp.concatenate([fq[t, s, :] for t in range(4)], axis=1).astype(BF16)
         qb = fq[4, s, :][:, 0:64].astype(BF16)
-        v = dot(qa, kv[ik, 0:512, :]) + dot(qb, kv[ik, 512:576, :])
-        ok = (lane16 >= lo) & (lane16 < hi)
+        kk = jnp.concatenate([kv[one], kv[two]], axis=1)
+        v = dot(qa, kk[0:512, :]) + dot(qb, kk[512:576, :])
+        ok = (spot >= lo) & (spot < hi)
         v = jnp.where(ok, v, NEG)
         m = jnp.max(v, axis=1, keepdims=True)
         w = jnp.where(ok, jnp.exp(v - m), 0.0).astype(BF16)
         den = jnp.sum(w.astype(F32), axis=1, keepdims=True)
-        num = dot_nt(w, kv[ik, 0:512, :])
-        o = pl.ds(pl.multiple_of(i * 16, 16), 16)
-        mb[o, :] = jnp.broadcast_to(m, (16, 128))
-        db[o, :] = jnp.broadcast_to(den, (16, 128))
+        num = dot_nt(w, kk[0:512, :])
+        mb[s, :] = jnp.broadcast_to(m, (32, 128))
+        db[s, :] = jnp.broadcast_to(den, (32, 128))
         for t in range(4):
-            nb[t, o, :] = num[:, t * 128 : (t + 1) * 128]
-
-    for k in range(4):
-        page(pages + k, pages, k, k + 1)
+            nb[t, s, :] = num[:, t * 128 : (t + 1) * 128]
+
+    for k in (0, 2):
+        pair(pages + k, pages, pages, group + k, group + k + 1)
     for cp in kl:
         cp.wait()
 
     @pl.loop(0, pages // 8)
     def _(g):
-        for u in range(8):
+        for u in range(0, 8, 2):
             i = g * 8 + u
-            page(i, i, 0, meta_v[pl.ds(i, 1), :])
+            hi = [jnp.broadcast_to(meta_v[pl.ds(i + n, 1), :], (16, 128)) for n in range(2)]
+            hi = jnp.concatenate(hi, axis=0)
+            pair(i, i, i + 1, 0, jnp.concatenate([hi, hi], axis=1))
 
     if STOP == 3:
         return bail(*[wl[i] for i in range(1, 9)], *gc)
@@ -405,14 +431,13 @@
     shin[...] = (ga / (1.0 + jnp.exp(-ga)) * ua).astype(BF16)
 
     gm = gates[...].reshape(512, 128)
-    ids = lax.broadcasted_iota(jnp.int32, (128, 176), 0) % 64
-
-    @pl.loop(0, 4)
-    def _(e):
-        ga = dot_nt(xm[...], wg[e])
-        ua = dot_nt(xm[...], wu[e])
-        gw = dot(gm, jnp.where(ids == me * 4 + e, 1.0, 0.0).astype(BF16))
-        inner[e] = (ga / (1.0 + jnp.exp(-ga)) * ua * gw).astype(BF16)
+    for lo, hi in ((0, 256), (256, 512), (512, 704)):
+        ga = dot_nt(xm[...], wg[lo:hi, :])
+        ua = dot_nt(xm[...], wu[lo:hi, :])
+        ids = lax.broadcasted_iota(jnp.int32, (128, hi - lo), 0) % 64
+        unit = lax.broadcasted_iota(jnp.int32, (128, hi - lo), 1) + lo
+        gw = dot(gm, jnp.where(ids == me * 4 + unit // 176, 1.0, 0.0).astype(BF16))
+        inner[:, lo:hi] = (ga / (1.0 + jnp.exp(-ga)) * ua * gw).astype(BF16)
 
     if STOP == 10:
         return bail()
@@ -424,9 +449,7 @@
     def down(t, half):
         wdt = WIDTHS[t]
         cols = pl.ds(pl.multiple_of(half * 1024 + STARTS[t], 128), wdt)
-        v = dot(inner[0], wd[0, :, cols])
-        for e in range(1, 4):
-            v = v + dot(inner[e], wd[e, :, cols])
+        v = dot(inner[...], wd[:, cols])
         sh = dot(shin[...], sd[:, cols])
         ys[t][...] = v.reshape(4, 4, 4, 8, wdt)
         ys[t][x, z] = ys[t][x, z] + sh.reshape(4, 8, wdt)
@@ -498,7 +521,7 @@
 def scratch():
     v = pltpu.VMEM
     i32 = jnp.int32
-    big = [v((4, 176, 2048), BF16)] * 3 + [v((352, 2048), BF16)] * 3
+    big = [v((704, 2048), BF16)] * 3 + [v((352, 2048), BF16)] * 3
     out = [v((16, 128, 512), BF16), v((16, 512, 128), BF16), v((49, 576, 128), BF16), v((256, 2048), BF16)]
     out += big + [dma(9), dma(6)]
     out += [
@@ -509,13 +532,13 @@
         v((16, 4, 128), F32), dma(2, 16),
     ]
     out += [
-        v((16, 4, 2048), BF16), v((16, 4, 128), F32), v((16, 32, 128), BF16), v((4, 2048), F32),
+        v((16, 4, 2048), BF16), v((16, 4, 128), F32), v((32, 128), BF16), v((16, 32, 128), BF16), v((4, 2048), F32),
         v((8, 4, 256), BF16), v((8, 4, 256), BF16), v((32, 256), F32), v((32, 2048), F32),
         v((8, 4, 2048), BF16), v((8, 4, 2048), BF16), v((4, 2048), BF16), v((4, 2048), BF16),
         v((8, 2048), F32),
     ]
     out += [v((2, 4, 4, 4, 8, w), BF16) for w in WIDTHS]
-    out += [v((512, 2048), BF16), v((4, 512, 176), BF16), v((32, 352), BF16)]
+    out += [v((512, 2048), BF16), v((512, 704), BF16), v((32, 352), BF16)]
     out += [v((4, 4, 4, 8, w), F32) for w in WIDTHS]
     out += [v((4, 4, 4, 8, w), BF16) for w in WIDTHS] * 3
 
@@ -536,17 +559,17 @@
     return pltpu.CompilerParams(vmem_limit_bytes=LIMIT, collective_id=cid, has_side_effects=True)
 
 
-def call(q, table, lens, new, hid, gain, gates, *weights):
+def call(q, table, lens, new, hid, gain, routes, gates, *weights):
     sds = jax.ShapeDtypeStruct
     return pl.pallas_call(
         layer,
         out_shape=(sds((4, 2048), F32), sds((4, 2048), F32)),
-        in_specs=[VM] * 7 + [HBM] * 10,
+        in_specs=[VM] * 8 + [HBM] * 10,
         out_specs=(VM, VM),
         scratch_shapes=scratch(),
         compiler_params=params(0),
         name="layer",
-    )(q, table, lens, new, hid, gain, gates, *weights)
+    )(q, table, lens, new, hid, gain, routes, gates, *weights)
 
 
 def shards(
@@ -569,18 +592,12 @@
     shared_up,
     shared_down,
 ):
-    experts = jnp.arange(64, dtype=jnp.int32)
-    dense = jnp.sum(
-        jnp.where(routes[0].reshape(32, 6)[:, :, None] == experts, gate_weights[0].reshape(32, 6)[:, :, None], 0.0),
-        axis=1,
-    )
-    coarse = dense.astype(BF16)
-    gates = jnp.concatenate([coarse, (dense - coarse.astype(F32)).astype(BF16)], axis=1)
-
     wide = lambda w: jnp.swapaxes(w, -1, -2)
+    flat = lambda w: w.reshape(-1, w.shape[-1])
     proj, moe = call(
-        queries[0], block_table[0], seq_lens, new_kv[0], hidden[0], norm_gain[None], gates,
-        w_uk, w_uv, wide(kv_cache[0]), o_proj, wide(w_gate), wide(w_up), w_down,
+        queries[0], block_table[0], seq_lens, new_kv[0], hidden[0], norm_gain[None],
+        routes[0].T, gate_weights[0].T,
+        w_uk, w_uv, wide(kv_cache[0]), o_proj, flat(wide(w_gate)), flat(wide(w_up)), flat(w_down),
         wide(shared_gate), wide(shared_up), shared_down,
     )
     layer_out = (hidden[0].astype(F32) + proj + moe).astype(BF16)

time: 99.3 us -> 87.9 us (0.89)
  Pallas kernels: 94.3 us -> 85.5 us
  local copies, waits for them, and re-layouts: 1.78 us -> 0.01 us
    pallas_call x1, Pallas kernels: 94.3 us -> 85.5 us  [call(): pl.pallas_call(layer, out_shape=(sds((4, 2048), F32), sds((4, 2048), F32)...]
    unnamed x4 -> x2, local copies, waits for them, and re-layouts: 1.63 us -> 0.01 us
where the time goes in v3:
time: 87.9 us; the launch traced here: 87.6 us
  Pallas kernels  85.5 us (97%)
  other arithmetic  1.46 us (2%)
    pallas_call x1, Pallas kernels, call(): pl.pallas_call(layer, out_shape=(sds((4, 2048), F32), sds((4, 2048), F32)...  85.5 us

profile of v3, /device:TPU:1, one launch (start us, length us, event | category | flops | bytes accessed | tf_op | source)
XLA Modules:
  0.0 87.6 jit_solution(1303200511377522568)
XLA Ops:
  0.6 0.0 copy-start
  0.6 85.5 %layer.1 = (f32[4,2048]{1,0:T(4,128)}, f32[4,2048]{1,0:T(4,128)}) custom-call(bf16[4,16,192]{2,1,0:T(8,128)(2,1)} %bitcast.35, s32[64,128]{1,0:T(8,128)} %bitcast.36, s32[1,64]{1,0:T(1,128)} %len_in.1, bf16[4,576]{1,0:T(4,128)(2,1)} %bitcast.40, bf16[4,2048]{1,0:T(4,128)(2,1)} %bitcast.34, f32[1,2048]{1,0:T(1,128)} %bitcast.39, s32[6,4,8]{2,1,0:T(4,128)} %bitcast.37, ...), custom_call_target="tpu_custom_call" | custom-call | tf_op jit(solution)/shard_map/layer/pallas_call | solution.py:564
  86.2 0.0 copy-done
  86.2 1.5 %fusion = (bf16[1,4,2048]{2,1,0:T(4,128)(2,1)}, bf16[1,4,2048]{2,1,0:T(4,128)(2,1)}) fusion(f32[4,2048]{1,0:T(4,128)} %get-tuple-element.5, f32[4,2048]{1,0:T(4,128)} %get-tuple-element.4, bf16[1,4,2048]{2,1,0:T(4,128)(2,1)S(1)} %copy-done), kind=kLoop, calls=%fused_computation.1 | loop fusion | flops 40960 | bytes 114688 | tf_op jit(solution)/shard_map/broadcast_in_dim | solution.py:604
Async XLA Ops:
  0.6 85.5 %copy-start = (bf16[1,4,2048]{2,1,0:T(4,128)(2,1)S(1)}, bf16[1,4,2048]{2,1,0:T(4,128)(2,1)}, u32[]{:S(2)}) copy-start(bf16[1,4,2048]{2,1,0:T(4,128)(2,1)} %param.18) | copy-start | bytes 49156

commit v4 on v3

--- a/solution.py
+++ b/solution.py
@@ -11,7 +11,6 @@
 BF16 = jnp.bfloat16
 NEG = -1e30
 EPS = 1e-06
-STOP = 99
 NX = 4
 MESH = pl.DeviceIdType.MESH
 VM = pl.BlockSpec(memory_space=pltpu.VMEM)
@@ -62,6 +61,11 @@
     )
     cp.start()
     return cp
+
+
+def settle(ref, *sems):
+    for sem in sems:
+        pltpu.make_async_copy(ref, ref, sem).wait()
 
 
 def hail(devices):
@@ -100,7 +104,8 @@
     reps = rep_peers(y, c)
     mate = y * 2 + 1 - c
     xs = (x0, x1, x2)
-    pages, chunk, rows = 48, 8, 64
+    ras, rbs = (ra0, ra1, ra2), (rb0, rb1, rb2)
+    pages, rows = 48, 64
     scale = 192 ** (-0.5)
 
     def load(h, v, sem):
@@ -109,10 +114,8 @@
         return cp
 
     wl = {0: load(wuk_h, wuk, wsem.at[0])}
-    kl = []
-    for i in range(pages // chunk):
-        s = pl.ds(i * chunk, chunk)
-        kl.append(load(cache.at[s], kv.at[s], kvsem.at[i]))
+    kl = load(cache, kv.at[pl.ds(0, pages)], kvsem)
+
     def peer(**over):
         at = {a: (coord[a] + over.get(a, 0)) % 4 for a in "xzy"}
         return {"pool": at["x"] * 4 + at["z"], "rep": at["y"] * 2 + c}
@@ -122,12 +125,6 @@
             ((wuv_h, wuv), (oproj_h, oproj), (sg_h, sg), (su_h, su), (sd_h, sd), (wg_h, wg), (wu_h, wu), (wd_h, wd))
         ):
             wl[i + 1] = load(h, v, wsem.at[i + 1])
-
-    def bail(*waits):
-        for cp in waits:
-            cp.wait()
-        proj_out[...] = jnp.zeros((4, 2048), F32)
-        moe_out[...] = jnp.zeros((4, 2048), F32)
 
     known = (
         [{"pool": q, "rep": rp_me} for _, q in pools]
@@ -172,13 +169,10 @@
     gates_own[...] = jnp.concatenate([coarse, fine], axis=1).astype(BF16)
 
     meet(known)
-    if STOP == 0:
-        return bail(*wl.values(), *kl)
-
-    first = [send(qp, qg.at[x, z], qsem.at[0, d], qsem.at[1, d], pool=q) for d, q in pools]
-    qg[x, z] = qp[...]
-    if STOP == 20:
-        return bail(*wl.values(), *kl, *first)
+
+    for _, q in pools:
+        send(qp, qg.at[me], qsem.at[0], qsem.at[1], pool=q)
+    qg[me] = qp[...]
 
     wide[...] = jnp.zeros((128, 640), F32)
     wide[0:4, 0:576] = new_in[...].astype(F32)
@@ -190,17 +184,15 @@
     for t in range(4):
         nb[t, pages * 16 + 64 :, :] = jnp.zeros(((rows - pages - 4) * 16, 128), F32)
 
-    for cp in first:
-        cp.wait()
-    gc = [send(gates_own, gates.at[me], gsem.at[0, d], gsem.at[1, d], pool=q) for d, q in pools]
+    settle(qg.at[pl.ds(0, 15)], qsem.at[0], qsem.at[1])
+    for _, q in pools:
+        send(gates_own, gates.at[me], gsem.at[0], gsem.at[1], pool=q)
     gates[me] = gates_own[...]
     wl[0].wait()
-    if STOP == 1:
-        return bail(*kl, *gc)
 
     @pl.loop(0, 64, unroll=4)
     def _(j):
-        v = qg[j // 16, (j // 4) % 4, j % 4].astype(F32)
+        v = qg[j // 4, j % 4].astype(F32)
         qf[pl.ds(pl.multiple_of(j * 16, 16), 16), :] = v[0:16]
         qr[pl.ds(pl.multiple_of(j * 8, 8), 8), :] = v[16:24]
 
@@ -215,8 +207,6 @@
         if h >= 8:
             b = jnp.concatenate([b[:, 64:128], b[:, 0:64]], axis=1)
         fq[4, s, :] = b
-    if STOP == 2:
-        return bail(*kl, *gc)
     more()
     group = lax.broadcasted_iota(jnp.int32, (32, 256), 0) // 16
     spot = lax.broadcasted_iota(jnp.int32, (32, 256), 1) - group * 128
@@ -240,8 +230,7 @@
 
     for k in (0, 2):
         pair(pages + k, pages, pages, group + k, group + k + 1)
-    for cp in kl:
-        cp.wait()
+    kl.wait()
 
     @pl.loop(0, pages // 8)
     def _(g):
@@ -251,8 +240,6 @@
             hi = jnp.concatenate(hi, axis=0)
             pair(i, i, i + 1, 0, jnp.concatenate([hi, hi], axis=1))
 
-    if STOP == 3:
-        return bail(*[wl[i] for i in range(1, 9)], *gc)
 
     m = jnp.full((rows, 128), NEG, F32)
     d = jnp.zeros((rows, 128), F32)
@@ -291,14 +278,12 @@
     for k in range(16):
         pbuf[k] = of[k * 4 : (k + 1) * 4, :].astype(BF16)
         stbuf[k] = sf[k * 4 : (k + 1) * 4, :]
-    if STOP == 4:
-        return bail(*[wl[i] for i in range(2, 9)], *gc)
-    sc = [send(stbuf.at[q], rst.at[me], ssem.at[0, d], ssem.at[1, d], pool=q) for d, q in pools]
-    pc = [send(pbuf.at[q], rp.at[me], psem.at[0, d], psem.at[1, d], pool=q) for d, q in pools]
+    for _, q in pools:
+        send(stbuf.at[q], rst.at[me], ssem.at[0], ssem.at[1], pool=q)
+        send(pbuf.at[q], rp.at[me], psem.at[0], psem.at[1], pool=q)
     rst[me] = stbuf[me]
     rp[me] = pbuf[me]
-    for cp in sc:
-        cp.wait()
+    settle(rst.at[pl.ds(0, 15)], ssem.at[0], ssem.at[1])
     top = rst[0]
     for s in range(1, 16):
         top = jnp.maximum(top, rst[s])
@@ -308,8 +293,7 @@
         rst[s] = e
         tot = tot + e
     inv = 1.0 / tot
-    for cp in pc:
-        cp.wait()
+    settle(rp.at[pl.ds(0, 15)], psem.at[0], psem.at[1])
 
     heads[...] = jnp.zeros((4, 2048), F32)
 
@@ -320,26 +304,22 @@
             cols = slice(h * 128, (h + 1) * 128)
             heads[:, cols] = heads[:, cols] + w[:, h : h + 1] * rp[s, :, cols].astype(F32)
 
-    if STOP == 5:
-        return bail(*[wl[i] for i in range(2, 9)], *gc)
     for g in range(8):
         hs[g] = heads[:, g * 256 : (g + 1) * 256].astype(BF16)
-    hc = [send(hs.at[q], hb.at[rp_me], hsem.at[0, d], hsem.at[1, d], rep=q) for d, q in reps]
+    for _, q in reps:
+        send(hs.at[q], hb.at[rp_me], hsem.at[0], hsem.at[1], rep=q)
     hb[rp_me] = hs[rp_me]
     wl[2].wait()
-    for cp in hc:
-        cp.wait()
-    if STOP == 6:
-        return bail(*[wl[i] for i in range(3, 9)], *gc)
+    settle(hb.at[pl.ds(0, 7)], hsem.at[0], hsem.at[1])
     for g in range(8):
         hbf[g * 4 : (g + 1) * 4, :] = hb[g].astype(F32)
     pf[...] = dot(hbf[...].astype(BF16), oproj[...])
     for g in range(8):
         ps[g] = pf[g * 4 : (g + 1) * 4, :].astype(BF16)
-    oc = [send(ps.at[q], pr.at[rp_me], osem.at[0, d], osem.at[1, d], rep=q) for d, q in reps]
+    for _, q in reps:
+        send(ps.at[q], pr.at[rp_me], osem.at[0], osem.at[1], rep=q)
     pr[rp_me] = ps[rp_me]
-    for cp in oc:
-        cp.wait()
+    settle(pr.at[pl.ds(0, 7)], osem.at[0], osem.at[1])
     proj = pr[0].astype(F32)
     for g in range(1, 8):
         proj = proj + pr[g].astype(F32)
@@ -348,12 +328,9 @@
     ms = jnp.mean(res * res, axis=1, keepdims=True)
     normed = (res * lax.rsqrt(ms + EPS) * gain[...]).astype(BF16)
 
-    if STOP == 7:
-        return bail(*[wl[i] for i in range(3, 9)], *gc)
     nown[...] = normed
     cp = send(nown, npart, nsem.at[0], nsem.at[1], rep=mate)
-    for g in gc:
-        g.wait()
+    settle(gates.at[pl.ds(0, 15)], gsem.at[0], gsem.at[1])
     cp.wait()
     mine = normed.astype(F32)
     theirs = npart[...].astype(F32)
@@ -363,8 +340,6 @@
         s = pl.ds(pl.multiple_of(c * 1024 + STARTS[t], 128), WIDTHS[t])
         xs[t][c, x, z, y] = blk[:, s].astype(BF16)
 
-    if STOP == 8:
-        return bail(*[wl[i] for i in range(3, 9)])
     whole = pl.ds(0, 4)
 
     def idx(at):
@@ -373,48 +348,39 @@
     def near(a, d):
         return (coord[a] + d) % 4
 
-    fwd = []
-
-    def share(t, k, at):
+    def share(t, at):
         ref = xs[t].at[(c,) + idx(at)]
-        fwd.append(send(ref, ref, fsem.at[0, t, k], fsem.at[1, t, k], rep=mate))
-
-    flat = {}
+        send(ref, ref, fsem.at[0, t], fsem.at[1, t], rep=mate)
+
     for da in STEPS:
         for db in STEPS:
             if da or db:
                 for t in range(3):
                     a, b, _ = ORDERS[t]
                     ref = xs[t].at[(c,) + idx(coord)]
-                    k = da * 4 + db
-                    flat[t, k] = send(
-                        ref, ref, asem.at[0, t, k], asem.at[1, t, k], **peer(**{a: da, b: db})
-                    )
-    last = {}
+                    send(ref, ref, asem.at[t, 4], asem.at[t, da], **peer(**{a: da, b: db}))
     for da in STEPS:
         for t in range(3):
             a, b, w = ORDERS[t]
-            for db in range(4):
-                if da or db:
-                    flat[t, da * 4 + db].wait()
-            at = {a: near(a, -da), b: whole, w: coord[w]}
-            ref = xs[t].at[(c,) + idx(at)]
+            some = pl.ds(0, 4 if da else 3)
+            settle(xs[t].at[(c,) + idx({a: near(a, -da), b: some, w: coord[w]})], asem.at[t, da])
+            ref = xs[t].at[(c,) + idx({a: near(a, -da), b: whole, w: coord[w]})]
             for d in range(1, 4):
-                k = da * 4 + d
-                last[t, da, d] = send(ref, ref, bsem.at[0, t, k], bsem.at[1, t, k], **peer(**{w: d}))
+                send(ref, ref, bsem.at[t, 0], bsem.at[t, d], **peer(**{w: d}))
     for t in range(3):
         a, b, w = ORDERS[t]
-        share(t, 0, {a: whole, b: whole, w: coord[w]})
+        share(t, {a: whole, b: whole, w: coord[w]})
     for d in (1, 3, 2):
         for t in range(3):
             a, b, w = ORDERS[t]
-            for da in STEPS:
-                last[t, da, d].wait()
-            share(t, d, {a: whole, b: whole, w: near(w, -d)})
-    for cp in fwd:
-        cp.wait()
-    if STOP == 9:
-        return bail(*[wl[i] for i in range(3, 9)])
+            at = {a: whole, b: whole, w: near(w, -d)}
+            settle(xs[t].at[(c,) + idx(at)], bsem.at[t, d])
+            share(t, at)
+    for t in range(3):
+        a, b, w = ORDERS[t]
+        settle(rbs[t].at[pl.ds(0, 15)], asem.at[t, 4])
+        settle(xs[t].at[(c,) + idx({a: whole, b: whole, w: pl.ds(0, 3)})], bsem.at[t, 0])
+        settle(xs[t].at[c], fsem.at[0, t], fsem.at[1, t])
 
     for t in range(3):
         for h in range(2):
@@ -439,8 +405,6 @@
         gw = dot(gm, jnp.where(ids == me * 4 + unit // 176, 1.0, 0.0).astype(BF16))
         inner[:, lo:hi] = (ga / (1.0 + jnp.exp(-ga)) * ua * gw).astype(BF16)
 
-    if STOP == 10:
-        return bail()
     ys = (y0, y1, y2)
     css = (cs0, cs1, cs2)
     crs = (cr0, cr1, cr2)
@@ -460,10 +424,8 @@
         cc.append(send(css[t], crs[t], csem.at[0, t], csem.at[1, t], rep=mate))
 
     sbs = (sb0, sb1, sb2)
-    ras, rbs = (ra0, ra1, ra2), (rb0, rb1, rb2)
 
     back = (2, 1, 3, 0)
-    away = {}
     for t in range(3):
         down(t, c)
         cc[t].wait()
@@ -475,18 +437,12 @@
             for d in range(1, 4):
                 src = sbs[t].at[idx({a: near(a, da), b: whole, w: near(w, d)})]
                 dst = ras[t].at[(d,) + idx({a: near(a, da), b: whole, w: coord[w] * 0})]
-                k = da * 4 + d
-                away[t, da, d] = send(src, dst, dsem.at[0, t, k], dsem.at[1, t, k], **peer(**{w: d}))
-    if STOP == 11:
-        return bail(*away.values())
-    home = {}
-    own = {}
+                send(src, dst, dsem.at[t, 4], dsem.at[t, da], **peer(**{w: d}))
     for da in back:
         for t in range(3):
             a, b, w = ORDERS[t]
-            for d in range(1, 4):
-                away[t, da, d].wait()
             at = idx({a: near(a, da), b: whole, w: coord[w] * 0})
+            settle(ras[t].at[(pl.ds(1, 3),) + at], dsem.at[t, da])
             v = ys[t][idx({a: near(a, da), b: whole, w: coord[w]})]
             for d in range(1, 4):
                 v = v + ras[t][(d,) + at].astype(F32)
@@ -496,12 +452,13 @@
                 if k:
                     ref = ras[t].at[(0,) + idx({a: near(a, da), b: near(b, db), w: coord[w] * 0})]
                     dst = rbs[t].at[(k,) + (pl.ds(0, 1),) * 3]
-                    home[t, k] = send(ref, dst, esem.at[0, t, k], esem.at[1, t, k], **peer(**{a: da, b: db}))
+                    send(ref, dst, esem.at[0, t], esem.at[1, t], **peer(**{a: da, b: db}))
     for t in range(3):
         a, b, w = ORDERS[t]
         v = ras[t][(0,) + idx({a: coord[a], b: coord[b], w: coord[w] * 0})].astype(F32)
+        settle(rbs[t].at[pl.ds(1, 15)], esem.at[0, t], esem.at[1, t])
+        settle(ras[t].at[pl.ds(1, 3)], dsem.at[t, 4])
         for k in range(1, 16):
-            home[t, k].wait()
             v = v + rbs[t][k].astype(F32)
         blk[:, STARTS[t] : STARTS[t] + WIDTHS[t]] = v.reshape(8, WIDTHS[t])
     lo, hi = blk[0:4, 0:1024], blk[4:8, 0:1024]
@@ -523,13 +480,13 @@
     i32 = jnp.int32
     big = [v((704, 2048), BF16)] * 3 + [v((352, 2048), BF16)] * 3
     out = [v((16, 128, 512), BF16), v((16, 512, 128), BF16), v((49, 576, 128), BF16), v((256, 2048), BF16)]
-    out += big + [dma(9), dma(6)]
+    out += big + [dma(9), pltpu.SemaphoreType.DMA]
     out += [
-        v((4, 24, 128), BF16), v((4, 4, 4, 24, 128), BF16), v((1024, 128), F32), v((512, 128), F32),
+        v((4, 24, 128), BF16), v((16, 4, 24, 128), BF16), v((1024, 128), F32), v((512, 128), F32),
         v((5, 1024, 128), F32), v((4, 1024, 128), F32), v((1024, 128), F32), v((1024, 128), F32),
         v((64, 128), i32), v((64, 128), i32), v((128, 640), F32),
         v((64, 2048), BF16), v((64, 2048), F32), v((64, 128), F32), v((16, 4, 2048), BF16),
-        v((16, 4, 128), F32), dma(2, 16),
+        v((16, 4, 128), F32), dma(2),
     ]
     out += [
         v((16, 4, 2048), BF16), v((16, 4, 128), F32), v((32, 128), BF16), v((16, 32, 128), BF16), v((4, 2048), F32),
@@ -549,8 +506,8 @@
     out += [v((16, 1, 1, 1, 8, w), BF16) for w in WIDTHS]
     out += [v((4, 1024), BF16), v((4, 1024), BF16)]
     out += [
-        dma(2, 16), dma(2, 16), dma(2, 16), dma(2, 8), dma(2, 8), dma(2),
-        dma(2, 3, 16), dma(2, 3, 16), dma(2, 3, 4), dma(2, 3), dma(2, 3, 16), dma(2, 3, 16), dma(2),
+        dma(2), dma(2), dma(2), dma(2), dma(2), dma(2),
+        dma(3, 5), dma(3, 4), dma(2, 3), dma(2, 3), dma(3, 5), dma(2, 3), dma(2),
     ]
     return out
 

time: 87.9 us -> 82.8 us (0.942)
  Pallas kernels: 85.5 us -> 80.4 us
    pallas_call x1, Pallas kernels: 85.5 us -> 80.4 us  [call(): pl.pallas_call(layer, out_shape=(sds((4, 2048), F32), sds((4, 2048), F32)...]
where the time goes in v4:
time: 82.8 us; the launch traced here: 82.5 us
  Pallas kernels  80.4 us (97%)
  other arithmetic  1.46 us (2%)
    pallas_call x1, Pallas kernels, call(): pl.pallas_call(layer, out_shape=(sds((4, 2048), F32), sds((4, 2048), F32)...  80.4 us

profile of v4, /device:TPU:1, one launch (start us, length us, event | category | flops | bytes accessed | tf_op | source)
XLA Modules:
  0.0 82.5 jit_solution(8070000527174156267)
XLA Ops:
  0.6 0.0 copy-start
  0.6 80.4 %layer.1 = (f32[4,2048]{1,0:T(4,128)}, f32[4,2048]{1,0:T(4,128)}) custom-call(bf16[4,16,192]{2,1,0:T(8,128)(2,1)} %bitcast.35, s32[64,128]{1,0:T(8,128)} %bitcast.36, s32[1,64]{1,0:T(1,128)} %len_in.1, bf16[4,576]{1,0:T(4,128)(2,1)} %bitcast.40, bf16[4,2048]{1,0:T(4,128)(2,1)} %bitcast.34, f32[1,2048]{1,0:T(1,128)} %bitcast.39, s32[6,4,8]{2,1,0:T(4,128)} %bitcast.37, ...), custom_call_target="tpu_custom_call" | custom-call | tf_op jit(solution)/shard_map/layer/pallas_call | solution.py:521
  81.1 0.0 copy-done
  81.1 1.5 %fusion = (bf16[1,4,2048]{2,1,0:T(4,128)(2,1)}, bf16[1,4,2048]{2,1,0:T(4,128)(2,1)}) fusion(f32[4,2048]{1,0:T(4,128)} %get-tuple-element.5, f32[4,2048]{1,0:T(4,128)} %get-tuple-element.4, bf16[1,4,2048]{2,1,0:T(4,128)(2,1)S(1)} %copy-done), kind=kLoop, calls=%fused_computation.1 | loop fusion | flops 40960 | bytes 114688 | tf_op jit(solution)/shard_map/broadcast_in_dim | solution.py:561
Async XLA Ops:
  0.6 80.4 %copy-start = (bf16[1,4,2048]{2,1,0:T(4,128)(2,1)S(1)}, bf16[1,4,2048]{2,1,0:T(4,128)(2,1)}, u32[]{:S(2)}) copy-start(bf16[1,4,2048]{2,1,0:T(4,128)(2,1)} %param.18) | copy-start | bytes 49156

commit v5 on v4

--- a/solution.py
+++ b/solution.py
@@ -92,7 +92,7 @@
     wuk, wuv, kv, oproj, wg, wu, wd, sg, su, sd, wsem, kvsem,
     qp, qg, qf, qr, fq, nb, mb, db, mrow, meta_v, wide, vb, of, sf, pbuf, stbuf, qsem,
     rp, rst, gates_own, gates, heads, hs, hb, hbf, pf, ps, pr, nown, npart, blk,
-    x0, x1, x2, xm, inner, shin, y0, y1, y2, cs0, cs1, cs2, cr0, cr1, cr2,
+    x0, x1, x2, xm, gws, inner, shin, y0, y1, y2, cs0, cs1, cs2, cr0, cr1, cr2,
     sb0, sb1, sb2, ra0, ra1, ra2, rb0, rb1, rb2, fs, fr,
     psem, ssem, gsem, hsem, osem, nsem, asem, bsem, fsem, csem, dsem, esem, lsem,
 ):
@@ -232,10 +232,10 @@
         pair(pages + k, pages, pages, group + k, group + k + 1)
     kl.wait()
 
-    @pl.loop(0, pages // 8)
+    @pl.loop(0, pages // 16)
     def _(g):
-        for u in range(0, 8, 2):
-            i = g * 8 + u
+        for u in range(0, 16, 2):
+            i = g * 16 + u
             hi = [jnp.broadcast_to(meta_v[pl.ds(i + n, 1), :], (16, 128)) for n in range(2)]
             hi = jnp.concatenate(hi, axis=0)
             pair(i, i, i + 1, 0, jnp.concatenate([hi, hi], axis=1))
@@ -293,16 +293,15 @@
         rst[s] = e
         tot = tot + e
     inv = 1.0 / tot
+    shares = [rst[s] * inv for s in range(16)]
     settle(rp.at[pl.ds(0, 15)], psem.at[0], psem.at[1])
 
-    heads[...] = jnp.zeros((4, 2048), F32)
-
-    @pl.loop(0, 16)
-    def _(s):
-        w = rst[s] * inv
-        for h in range(16):
-            cols = slice(h * 128, (h + 1) * 128)
-            heads[:, cols] = heads[:, cols] + w[:, h : h + 1] * rp[s, :, cols].astype(F32)
+    for h in range(16):
+        cols = slice(h * 128, (h + 1) * 128)
+        v = jnp.zeros((4, 128), F32)
+        for s in range(16):
+            v = v + shares[s][:, h : h + 1] * rp[s, :, cols].astype(F32)
+        heads[:, cols] = v
 
     for g in range(8):
         hs[g] = heads[:, g * 256 : (g + 1) * 256].astype(BF16)
@@ -359,6 +358,11 @@
                     a, b, _ = ORDERS[t]
                     ref = xs[t].at[(c,) + idx(coord)]
                     send(ref, ref, asem.at[t, 4], asem.at[t, da], **peer(**{a: da, b: db}))
+    gm = gates[...].reshape(512, 128)
+    for lo, hi in ((0, 256), (256, 512), (512, 704)):
+        ids = lax.broadcasted_iota(jnp.int32, (128, hi - lo), 0) % 64
+        unit = lax.broadcasted_iota(jnp.int32, (128, hi - lo), 1) + lo
+        gws[:, lo:hi] = dot(gm, jnp.where(ids == me * 4 + unit // 176, 1.0, 0.0).astype(BF16))
     for da in STEPS:
         for t in range(3):
             a, b, w = ORDERS[t]
@@ -396,14 +400,10 @@
     ua = dot_nt(col, su[...])
     shin[...] = (ga / (1.0 + jnp.exp(-ga)) * ua).astype(BF16)
 
-    gm = gates[...].reshape(512, 128)
     for lo, hi in ((0, 256), (256, 512), (512, 704)):
         ga = dot_nt(xm[...], wg[lo:hi, :])
         ua = dot_nt(xm[...], wu[lo:hi, :])
-        ids = lax.broadcasted_iota(jnp.int32, (128, hi - lo), 0) % 64
-        unit = lax.broadcasted_iota(jnp.int32, (128, hi - lo), 1) + lo
-        gw = dot(gm, jnp.where(ids == me * 4 + unit // 176, 1.0, 0.0).astype(BF16))
-        inner[:, lo:hi] = (ga / (1.0 + jnp.exp(-ga)) * ua * gw).astype(BF16)
+        inner[:, lo:hi] = (ga / (1.0 + jnp.exp(-ga)) * ua * gws[:, lo:hi]).astype(BF16)
 
     ys = (y0, y1, y2)
     css = (cs0, cs1, cs2)
@@ -495,7 +495,7 @@
         v((8, 2048), F32),
     ]
     out += [v((2, 4, 4, 4, 8, w), BF16) for w in WIDTHS]
-    out += [v((512, 2048), BF16), v((512, 704), BF16), v((32, 352), BF16)]
+    out += [v((512, 2048), BF16), v((512, 704), F32), v((512, 704), BF16), v((32, 352), BF16)]
     out += [v((4, 4, 4, 8, w), F32) for w in WIDTHS]
     out += [v((4, 4, 4, 8, w), BF16) for w in WIDTHS] * 3
 

time: 82.8 us -> 81.4 us (0.983)
  Pallas kernels: 80.4 us -> 79 us
    pallas_call x1, Pallas kernels: 80.4 us -> 79 us  [call(): pl.pallas_call(layer, out_shape=(sds((4, 2048), F32), sds((4, 2048), F32)...]
where the time goes in v5:
time: 81.4 us; the launch traced here: 81.2 us
  Pallas kernels  79 us (97%)
  other arithmetic  1.46 us (2%)
    pallas_call x1, Pallas kernels, call(): pl.pallas_call(layer, out_shape=(sds((4, 2048), F32), sds((4, 2048), F32)...  79 us

profile of v5, /device:TPU:1, one launch (start us, length us, event | category | flops | bytes accessed | tf_op | source)
XLA Modules:
  0.0 81.2 jit_solution(12158728139636490562)
XLA Ops:
  0.6 0.0 copy-start
  0.6 79.0 %layer.1 = (f32[4,2048]{1,0:T(4,128)}, f32[4,2048]{1,0:T(4,128)}) custom-call(bf16[4,16,192]{2,1,0:T(8,128)(2,1)} %bitcast.35, s32[64,128]{1,0:T(8,128)} %bitcast.36, s32[1,64]{1,0:T(1,128)} %len_in.1, bf16[4,576]{1,0:T(4,128)(2,1)} %bitcast.40, bf16[4,2048]{1,0:T(4,128)(2,1)} %bitcast.34, f32[1,2048]{1,0:T(1,128)} %bitcast.39, s32[6,4,8]{2,1,0:T(4,128)} %bitcast.37, ...), custom_call_target="tpu_custom_call" | custom-call | tf_op jit(solution)/shard_map/layer/pallas_call | solution.py:521
  79.7 0.0 copy-done
  79.7 1.5 %fusion = (bf16[1,4,2048]{2,1,0:T(4,128)(2,1)}, bf16[1,4,2048]{2,1,0:T(4,128)(2,1)}) fusion(f32[4,2048]{1,0:T(4,128)} %get-tuple-element.5, f32[4,2048]{1,0:T(4,128)} %get-tuple-element.4, bf16[1,4,2048]{2,1,0:T(4,128)(2,1)S(1)} %copy-done), kind=kLoop, calls=%fused_computation.1 | loop fusion | flops 40960 | bytes 114688 | tf_op jit(solution)/shard_map/broadcast_in_dim | solution.py:561
Async XLA Ops:
  0.6 79.0 %copy-start = (bf16[1,4,2048]{2,1,0:T(4,128)(2,1)S(1)}, bf16[1,4,2048]{2,1,0:T(4,128)(2,1)}, u32[]{:S(2)}) copy-start(bf16[1,4,2048]{2,1,0:T(4,128)(2,1)} %param.18) | copy-start | bytes 49156

commit v6 on v5

--- a/solution.py
+++ b/solution.py
@@ -86,10 +86,10 @@
 
 
 def layer(
-    q_in, table_in, len_in, new_in, hid, gain, routes_in, weights_in,
+    q_in, table_in, len_in, new_in, routes_in, weights_in, hid_h, gain_h,
     wuk_h, wuv_h, cache, oproj_h, wg_h, wu_h, wd_h, sg_h, su_h, sd_h,
     proj_out, moe_out,
-    wuk, wuv, kv, oproj, wg, wu, wd, sg, su, sd, wsem, kvsem,
+    wuk, wuv, kv, oproj, wg, wu, wd, sg, su, sd, hid, gain, wsem, kvsem,
     qp, qg, qf, qr, fq, nb, mb, db, mrow, meta_v, wide, vb, of, sf, pbuf, stbuf, qsem,
     rp, rst, gates_own, gates, heads, hs, hb, hbf, pf, ps, pr, nown, npart, blk,
     x0, x1, x2, xm, gws, inner, shin, y0, y1, y2, cs0, cs1, cs2, cr0, cr1, cr2,
@@ -122,7 +122,8 @@
 
     def more():
         for i, (h, v) in enumerate(
-            ((wuv_h, wuv), (oproj_h, oproj), (sg_h, sg), (su_h, su), (sd_h, sd), (wg_h, wg), (wu_h, wu), (wd_h, wd))
+            ((wuv_h, wuv), (oproj_h, oproj), (sg_h, sg), (su_h, su), (sd_h, sd), (wg_h, wg), (wu_h, wu), (wd_h, wd),
+             (hid_h, hid), (gain_h, gain))
         ):
             wl[i + 1] = load(h, v, wsem.at[i + 1])
 
@@ -232,10 +233,10 @@
         pair(pages + k, pages, pages, group + k, group + k + 1)
     kl.wait()
 
-    @pl.loop(0, pages // 16)
+    @pl.loop(0, pages // 24)
     def _(g):
-        for u in range(0, 16, 2):
-            i = g * 16 + u
+        for u in range(0, 24, 2):
+            i = g * 24 + u
             hi = [jnp.broadcast_to(meta_v[pl.ds(i + n, 1), :], (16, 128)) for n in range(2)]
             hi = jnp.concatenate(hi, axis=0)
             pair(i, i, i + 1, 0, jnp.concatenate([hi, hi], axis=1))
@@ -323,6 +324,8 @@
     for g in range(1, 8):
         proj = proj + pr[g].astype(F32)
     proj_out[...] = proj
+    wl[9].wait()
+    wl[10].wait()
     res = hid[...].astype(F32) + proj
     ms = jnp.mean(res * res, axis=1, keepdims=True)
     normed = (res * lax.rsqrt(ms + EPS) * gain[...]).astype(BF16)
@@ -480,7 +483,7 @@
     i32 = jnp.int32
     big = [v((704, 2048), BF16)] * 3 + [v((352, 2048), BF16)] * 3
     out = [v((16, 128, 512), BF16), v((16, 512, 128), BF16), v((49, 576, 128), BF16), v((256, 2048), BF16)]
-    out += big + [dma(9), pltpu.SemaphoreType.DMA]
+    out += big + [v((4, 2048), BF16), v((1, 2048), F32), dma(11), pltpu.SemaphoreType.DMA]
     out += [
         v((4, 24, 128), BF16), v((16, 4, 24, 128), BF16), v((1024, 128), F32), v((512, 128), F32),
         v((5, 1024, 128), F32), v((4, 1024, 128), F32), v((1024, 128), F32), v((1024, 128), F32),
@@ -516,17 +519,17 @@
     return pltpu.CompilerParams(vmem_limit_bytes=LIMIT, collective_id=cid, has_side_effects=True)
 
 
-def call(q, table, lens, new, hid, gain, routes, gates, *weights):
+def call(q, table, lens, new, routes, gates, *rest):
     sds = jax.ShapeDtypeStruct
     return pl.pallas_call(
         layer,
         out_shape=(sds((4, 2048), F32), sds((4, 2048), F32)),
-        in_specs=[VM] * 8 + [HBM] * 10,
+        in_specs=[VM] * 6 + [HBM] * 12,
         out_specs=(VM, VM),
         scratch_shapes=scratch(),
         compiler_params=params(0),
         name="layer",
-    )(q, table, lens, new, hid, gain, routes, gates, *weights)
+    )(q, table, lens, new, routes, gates, *rest)
 
 
 def shards(
@@ -552,8 +555,8 @@
     wide = lambda w: jnp.swapaxes(w, -1, -2)
     flat = lambda w: w.reshape(-1, w.shape[-1])
     proj, moe = call(
-        queries[0], block_table[0], seq_lens, new_kv[0], hidden[0], norm_gain[None],
-        routes[0].T, gate_weights[0].T,
+        queries[0], block_table[0], seq_lens, new_kv[0],
+        routes[0].T, gate_weights[0].T, hidden[0], norm_gain[None],
         w_uk, w_uv, wide(kv_cache[0]), o_proj, flat(wide(w_gate)), flat(wide(w_up)), flat(w_down),
         wide(shared_gate), wide(shared_up), shared_down,
     )

time: 81.4 us -> 81.5 us (level)
  no operation moved by 1% of the time
where the time goes in v6:
time: 81.5 us; the launch traced here: 81.2 us
  Pallas kernels  79.1 us (97%)
  other arithmetic  1.46 us (2%)
    pallas_call x1, Pallas kernels, call(): pl.pallas_call(layer, out_shape=(sds((4, 2048), F32), sds((4, 2048), F32)...  79.1 us

profile of v6, /device:TPU:1, one launch (start us, length us, event | category | flops | bytes accessed | tf_op | source)
XLA Modules:
  0.0 81.2 jit_solution(11183156846388839894)
XLA Ops:
  0.6 0.0 copy-start
  0.6 79.1 %layer.1 = (f32[4,2048]{1,0:T(4,128)}, f32[4,2048]{1,0:T(4,128)}) custom-call(bf16[4,16,192]{2,1,0:T(8,128)(2,1)} %bitcast.35, s32[64,128]{1,0:T(8,128)} %bitcast.36, s32[1,64]{1,0:T(1,128)} %len_in.1, bf16[4,576]{1,0:T(4,128)(2,1)} %bitcast.40, s32[6,4,8]{2,1,0:T(4,128)} %bitcast.37, f32[6,4,8]{2,1,0:T(4,128)} %bitcast.38, bf16[4,2048]{1,0:T(4,128)(2,1)} %bitcast.34, ...), custom_call_target="tpu_custom_call" | custom-call | tf_op jit(solution)/shard_map/layer/pallas_call | solution.py:524
  79.7 0.0 copy-done
  79.7 1.5 %fusion = (bf16[1,4,2048]{2,1,0:T(4,128)(2,1)}, bf16[1,4,2048]{2,1,0:T(4,128)(2,1)}) fusion(f32[4,2048]{1,0:T(4,128)} %get-tuple-element.5, f32[4,2048]{1,0:T(4,128)} %get-tuple-element.4, bf16[1,4,2048]{2,1,0:T(4,128)(2,1)S(1)} %copy-done), kind=kLoop, calls=%fused_computation.1 | loop fusion | flops 40960 | bytes 114688 | tf_op jit(solution)/shard_map/broadcast_in_dim | solution.py:564
Async XLA Ops:
  0.6 79.1 %copy-start = (bf16[1,4,2048]{2,1,0:T(4,128)(2,1)S(1)}, bf16[1,4,2048]{2,1,0:T(4,128)(2,1)}, u32[]{:S(2)}) copy-start(bf16[1,4,2048]{2,1,0:T(4,128)(2,1)} %param.18) | copy-start | bytes 49156
